TPU v7x, 32 devices: a whole 2x2x4 slice. The times are simulated.
32 devices in a mesh: groups: 2 (over y), visit: 4 (over z), strip: 2 (over x), band: 2 (over core).
Axes of the slice: x: 2, y: 2, z: 4, core: 2. Of those that a mesh axis runs over, the one named last changes fastest.
Arguments:
- images: bfloat16 [2, 128, 128, 256], P('band', ('groups', 'visit'), 'strip'), parts along dimension 1, may hold values from -8 to 8
- mask_bits: int32 [2, 128, 128, 256], P('band', ('groups', 'visit'), 'strip'), parts along dimension 1, may hold values from 0 to 15
- visit_weight: bfloat16 [2, 128], P('band', ('groups', 'visit')), parts along dimension 1, may hold values from 1 to 4
- intersection: int32 [128, 1], P(('groups', 'visit')), parts along dimension 0, may hold values from 0 to 3, as said below
- patch_owner: int32 [8], P('groups'), parts along dimension 0, may hold values from 0 to 3, each once
Outputs:
- coadd_image: bfloat16 [2, 8, 128, 256], P('band', ('groups', 'visit'), 'strip'), parts along dimension 1
- difference: bfloat16 [2, 128, 128, 256], P('band', ('groups', 'visit'), 'strip'), parts along dimension 1
There are 2 independent parts, one for each index of `groups`. A program takes and returns all parts, laid end to end along the dimension named above; each array names one. Nothing has to cross between parts.
Inputs may be any that keep to these rules, and one draw needn't show every extreme that they name: `intersection`: row j names the patch that piece j intersections. The 16 pieces of one visit index intersect 16 // 8 distinct patches, exactly 8 pieces each; one patch is intersected by 8 pieces of every visit index, and every patch is intersected by some piece. `patch_owner`: A permutation of the patches.
All inputs are finite; a program needn't handle non-finite values.
Results may differ from a plain program's by a relative error of at most 0.0071.
Values may be sent and summed in bfloat16 or wider, within the bound.
A program may use at most 64 MiB of HBM per device.

v0:
```python
import functools

import jax
import jax.numpy as jnp
import numpy as np
from jax import lax
from jax.experimental import pallas as pl
from jax.experimental.pallas import tpu as pltpu
from jax.sharding import PartitionSpec as P

BASES = 6
HALF = 9
TILE = 16

basis_rows = (0, 0, 1, 0, 2, 1)
basis_cols = (0, 1, 0, 2, 0, 1)
pairs = tuple((a, c) for a in range(BASES) for c in range(a, BASES))
MESH = pl.DeviceIdType.MESH
F32 = jnp.float32
BF16 = jnp.bfloat16


def kernel_taps():
    offsets = np.arange(2 * HALF + 1).astype(np.float32) - HALF
    gaussian = np.exp(-offsets * offsets / np.float32(18.0))
    centre = np.sum(offsets * offsets * gaussian * gaussian) / np.sum(gaussian * gaussian)
    table = np.stack([gaussian, offsets * gaussian, (offsets * offsets - centre) * gaussian])
    table = table / np.sqrt(np.sum(table * table, axis=1, keepdims=True))
    return table.astype(BF16).astype(np.float32)


def band_matrix(table, lead, trail, displace):
    index = np.arange(trail)[None, :] - np.arange(lead)[:, None] + displace
    inside = (index >= 0) & (index <= 2 * HALF)
    return np.where(inside[None], table[:, np.clip(index, 0, 2 * HALF)], 0.0)


def gather_matrix():
    result = np.zeros((BASES * 8, (len(pairs) + BASES) * TILE), np.float32)
    for n, (a, c) in enumerate(pairs):
        result[a * 8 + c, n * TILE : (n + 1) * TILE] = 1.0
        result[c * 8 + a, n * TILE : (n + 1) * TILE] = 1.0
    for a in range(BASES):
        n = len(pairs) + a
        result[a * 8 + 6, n * TILE : (n + 1) * TILE] = 1.0
    return result


def iota(shape, dim):
    return lax.broadcasted_iota(jnp.int32, shape, dim)


def nn(a, b):
    return jnp.dot(a, b, preferred_element_type=F32)


def nt(a, b, precision=None):
    return lax.dot_general(
        a, b, (((1,), (1,)), ((), ())), preferred_element_type=F32, precision=precision
    )


def kernel(
    visits, strips, distinct,
    images, masks, weight, cross, owner, cross_scalar, table_in,
    coadd_out, image_v, basis, mixers,
    mask_v, tables, use, use_image, send, recv, ids_own, ids, gath,
    prods, small, small_in,
    in_sem, const_sem, rs_send, rs_recv, id_send, id_recv, ag_send, ag_recv,
    halo_send, halo_recv,
    st_send, st_recv,
):
    pieces, rows, cols = images.shape[1:]
    blocks = rows // TILE
    span = pieces * TILE
    order = [0] + ([blocks - 1] if blocks > 1 else []) + list(range(1, blocks - 1))
    me = lax.axis_index("visit")
    strip = lax.axis_index("strip")

    loads = {}
    for t in order:
        piece_rows = pl.ds(t * TILE, TILE)
        loads[t] = ((
            pltpu.make_async_copy(masks.at[0, :, piece_rows, :], mask_v.at[t], in_sem.at[0, t]),
            pltpu.make_async_copy(images.at[0, :, piece_rows, :], image_v.at[t], in_sem.at[1, t]),
        ))
    constants = [pltpu.make_async_copy(table_in, tables, const_sem)]
    for t in order:
        for copy in loads[t]:
            copy.start()
    for copy in constants:
        copy.start()

    barrier = pltpu.get_barrier_semaphore()
    above = strip > 0
    below = strip < strips - 1

    def other_visit(k):
        return lax.rem(me + k, visits)

    for k in range(visits):
        for hop in range(strips):
            if k == 0 and hop == 0:
                continue
            target = {"visit": other_visit(k), "strip": lax.rem(strip + hop, strips)}
            pl.semaphore_signal(barrier, inc=1, device_id=target, device_id_type=MESH)

    seats = [owner[cross_scalar[0, j]] for j in range(pieces)]
    slots = [jnp.int32(0)] * distinct
    rank = jnp.int32(0)
    for q in range(visits):
        present = jnp.int32(0)
        for j in range(pieces):
            present = present | jnp.where(seats[j] == q, 1, 0)
        for d in range(distinct):
            slots[d] = slots[d] + jnp.where((present == 1) & (rank == d), q, 0)
        rank = rank + present

    position = jnp.zeros((1, pieces), jnp.int32)
    for p in range(visits):
        position = position + jnp.where(cross[...] == p, owner[p], 0)
    one_hot = (position == iota((128, pieces), 0)).astype(F32).astype(BF16)
    eq = jnp.concatenate([iota((TILE, 128), 1) == slots[d] for d in range(distinct)], axis=0)
    spread = nn(eq.astype(F32).astype(BF16), one_hot)
    spread = (spread * weight[...].astype(F32)).astype(BF16)
    e2 = iota((pieces, span), 0) == jnp.right_shift(iota((pieces, span), 1), 4)
    wide = nn(spread, e2.astype(F32).astype(BF16))
    same = (iota((distinct * TILE, span), 0) & (TILE - 1)) == (
        iota((distinct * TILE, span), 1) & (TILE - 1)
    )
    adder = jnp.where(same, wide, 0.0).astype(BF16)
    e_rows = jnp.right_shift(iota((span, 128), 0), 4) == iota((span, 128), 1)
    e_rows = e_rows.astype(F32).astype(BF16)
    row_hot = nt(e_rows[:, :pieces], one_hot)

    for t in order:
        for copy in loads[t]:
            copy.wait()
        usable = ((mask_v[t].reshape(span, cols) & 3) != 3).astype(F32).astype(BF16)
        masked = usable * image_v[t].reshape(span, cols)
        lanes = pl.ds(t * cols, cols)
        use[:, lanes] = usable
        use_image[:, lanes] = masked
        for part, value in enumerate((masked, usable)):
            total = nn(adder, value)
            for d in range(distinct):
                send[t, d, part] = total[d * TILE : (d + 1) * TILE].astype(BF16)
    names = jnp.zeros((1, 128), jnp.int32)
    for d in range(distinct):
        names = names + jnp.where(iota((1, 128), 1) == d, slots[d], 0)
    ids_own[...] = names.astype(F32)

    pl.semaphore_wait(barrier, visits * strips - 1)

    def block_of(r):
        return r ^ 1 if blocks % 2 == 0 else r

    my_block = me + 1 - 2 * lax.rem(me, 2) if blocks % 2 == 0 else me

    def reduce_copies(r, source):
        return (
            pltpu.make_async_remote_copy(
                src_ref=ids_own, dst_ref=ids.at[source],
                send_sem=id_send.at[r], recv_sem=id_recv.at[source],
                device_id={"visit": r}, device_id_type=MESH,
            ),
            pltpu.make_async_remote_copy(
                src_ref=send.at[block_of(r)], dst_ref=recv.at[source],
                send_sem=rs_send.at[r], recv_sem=rs_recv.at[source],
                device_id={"visit": r}, device_id_type=MESH,
            ),
        )

    def gather_copy(v, block):
        return pltpu.make_async_remote_copy(
            src_ref=gath.at[1 + block], dst_ref=gath.at[1 + block],
            send_sem=ag_send.at[v], recv_sem=ag_recv.at[block],
            device_id={"visit": v}, device_id_type=MESH,
        )

    for r in range(blocks):
        @pl.when(me != r)
        def _():
            for copy in reduce_copies(r, me):
                copy.start()

    @pl.when(jnp.logical_not(above))
    def _():
        gath[0] = jnp.zeros((visits, TILE, cols), BF16)

    @pl.when(jnp.logical_not(below))
    def _():
        gath[blocks + 1] = jnp.zeros((visits, TILE, cols), BF16)

    def reduce():
        recv[me] = send[my_block]
        ids[me] = ids_own[...]
        for v in range(visits):
            @pl.when(me != v)
            def _():
                for copy in reduce_copies(0, v):
                    copy.wait_recv()

        def one_patch(q, carry):
            numerator = jnp.zeros((TILE, cols), F32)
            denominator = jnp.zeros((TILE, cols), F32)
            number = lax.convert_element_type(q, F32)
            for v in range(visits):
                for d in range(distinct):
                    here = jnp.broadcast_to(ids[v][:, d : d + 1] == number, (TILE, cols))
                    numerator += jnp.where(here, recv[v, d, 0].astype(F32), 0.0)
                    denominator += jnp.where(here, recv[v, d, 1].astype(F32), 0.0)
            gath[1 + my_block, q] = (numerator / jnp.maximum(denominator, 1.0)).astype(BF16)
            return carry

        if visits <= 4:
            for q in range(visits):
                one_patch(q, 0)
        else:
            lax.fori_loop(0, visits, one_patch, 0)
        for v in range(visits):
            @pl.when(me != v)
            def _():
                gather_copy(v, my_block).start()

    if visits > blocks:
        pl.when(me < blocks)(reduce)
    else:
        reduce()

    for copy in constants:
        copy.wait()

    down = pltpu.make_async_remote_copy(
        src_ref=gath.at[blocks], dst_ref=gath.at[0],
        send_sem=halo_send.at[0], recv_sem=halo_recv.at[0],
        device_id={"strip": lax.rem(strip + 1, strips)}, device_id_type=MESH,
    )
    up = pltpu.make_async_remote_copy(
        src_ref=gath.at[1], dst_ref=gath.at[blocks + 1],
        send_sem=halo_send.at[1], recv_sem=halo_recv.at[1],
        device_id={"strip": lax.rem(strip + strips - 1, strips)}, device_id_type=MESH,
    )
    for t in [0, blocks - 1] + list(range(1, blocks - 1)):
        r = block_of(t)

        @pl.when(me != r)
        def _():
            gather_copy(r, t).wait_recv()

        if t == 0:
            pl.when(above)(up.start)
        if t == blocks - 1:
            pl.when(below)(down.start)
    pl.when(above)(down.wait_recv)
    pl.when(below)(up.wait_recv)
    for t in range(blocks):
        coadd_out[pl.ds(t * TILE, TILE), :] = gath[1 + t, me]

    top = BASES // 2 * cols
    vertical = tables[pl.ds(top, 3 * rows), pl.ds(0, rows + 2 * TILE)]
    top = top + 3 * rows

    def across(c):
        return tables[pl.ds(c * cols, cols), pl.ds(0, cols)]

    for d in range(distinct):
        template = jnp.concatenate([gath[i, slots[d]] for i in range(blocks + 2)], axis=0)
        smooth = nn(vertical, template).astype(BF16)
        planes = [None] * BASES
        for c in range(3):
            taken = [a for a in range(BASES) if basis_cols[a] == c]
            product = nn(smooth[: len(taken) * rows], across(c)).astype(BF16)
            for a in taken:
                r = basis_rows[a]
                planes[a] = product[r * rows : (r + 1) * rows]
        for a in range(BASES):
            for t in range(blocks):
                basis[d, pl.ds(a * TILE, TILE), pl.ds(t * cols, cols)] = planes[a][
                    t * TILE : (t + 1) * TILE
                ]
        for n, (a, c) in enumerate(pairs):
            product = planes[a] * planes[c]
            for t in range(blocks):
                prods[d, pl.ds(n * TILE, TILE), pl.ds(t * cols, cols)] = product[
                    t * TILE : (t + 1) * TILE
                ]

    def member(d):
        chosen = jnp.where(iota((span, 128), 1) == slots[d], row_hot, 0.0)
        return jnp.sum(chosen, axis=1, keepdims=True)

    def summed(values):
        return jnp.sum(values.reshape(pieces, TILE, values.shape[1]), axis=1)

    def keep(width):
        return (iota((span, width), 0) & (TILE - 1)) == (iota((span, width), 1) & (TILE - 1))

    wide_n = len(pairs) * TILE
    wide_b = BASES * TILE
    normal = jnp.zeros((pieces, wide_n), F32)
    right = jnp.zeros((pieces, wide_b), F32)
    for d in range(distinct):
        mine = member(d)
        normal = normal + summed(jnp.where(keep(wide_n), nt(use[...], prods[d]), 0.0) * mine)
        right = right + summed(jnp.where(keep(wide_b), nt(use_image[...], basis[d]), 0.0) * mine)
    normal_rows = tables[pl.ds(top, BASES * 8), pl.ds(0, wide_n)].astype(F32)
    right_rows = tables[pl.ds(top, BASES * 8), pl.ds(wide_n, wide_b)].astype(F32)
    system = nt(normal_rows, normal, lax.Precision.HIGHEST) + nt(
        right_rows, right, lax.Precision.HIGHEST
    )
    small[...] = jnp.concatenate(
        [system, jnp.zeros((BASES * 8, 128 - pieces), F32)], axis=1
    )
    exchanges = []
    for hop in range(1, strips):
        exchanges.append(pltpu.make_async_remote_copy(
            src_ref=small, dst_ref=small_in.at[hop - 1],
            send_sem=st_send.at[hop - 1], recv_sem=st_recv.at[hop - 1],
            device_id={"strip": lax.rem(strip + hop, strips)}, device_id_type=MESH,
        ))
    for copy in exchanges:
        copy.start()
    full = small[...]
    for hop in range(1, strips):
        exchanges[hop - 1].wait_recv()
        full = full + small_in[hop - 1]

    line = iota((8, 128), 0)
    table = [
        full[a * 8 : (a + 1) * 8] + jnp.where(line == a, 1.0, 0.0) for a in range(BASES)
    ]
    for column in range(BASES):
        pivot = table[column] / table[column][column : column + 1]
        for i in range(BASES):
            if i != column:
                table[i] = table[i] - table[i][column : column + 1] * pivot
        table[column] = pivot
    found = jnp.zeros((8, 128), F32)
    for a in range(BASES):
        found = found + jnp.where(line == a, table[a][BASES : BASES + 1], 0.0)
    high = found.astype(BF16).astype(F32)
    low = found - high
    both = jnp.concatenate([high, low], axis=0).astype(BF16)
    by_row = nt(e_rows, both).astype(BF16)
    wide_c = 2 * wide_b
    column = iota((16, wide_c), 1)
    source = jnp.where(
        column < wide_b, jnp.right_shift(column, 4), jnp.right_shift(column - wide_b, 4) + 8
    )
    e3 = (source == iota((16, wide_c), 0)).astype(F32).astype(BF16)
    mixer = jnp.where(keep(wide_c), nn(by_row, e3), 0.0)
    for d in range(distinct):
        mixers[d] = (mixer * member(d)).astype(BF16)

    for copy in exchanges:
        copy.wait_send()
    for r in range(blocks):
        @pl.when(me != r)
        def _():
            for copy in reduce_copies(r, me):
                copy.wait_send()

    def gathered():
        for v in range(visits):
            @pl.when(me != v)
            def _():
                gather_copy(v, my_block).wait_send()

    if visits > blocks:
        pl.when(me < blocks)(gathered)
    else:
        gathered()
    pl.when(below)(down.wait_send)
    pl.when(above)(up.wait_send)


def finish(coadd_in, image_v, basis, mixers, coadd_out, diff_out, diff_v, out_sem):
    distinct = basis.shape[0]
    blocks, pieces, _, cols = image_v.shape
    span = pieces * TILE
    stores = [pltpu.make_async_copy(coadd_in, coadd_out.at[0, 0], out_sem.at[0])]
    stores[0].start()
    for t in range(blocks):
        lanes = pl.ds(t * cols, cols)
        fitted = jnp.zeros((span, cols), F32)
        for d in range(distinct):
            planes = basis[d, :, lanes]
            fitted = fitted + nn(mixers[d], jnp.concatenate([planes, planes], axis=0))
        result = (image_v[t].reshape(span, cols).astype(F32) - fitted).astype(BF16)
        diff_v[t] = result.reshape(pieces, TILE, cols)
        copy = pltpu.make_async_copy(
            diff_v.at[t], diff_out.at[0, :, pl.ds(t * TILE, TILE), :], out_sem.at[1 + t]
        )
        copy.start()
        stores.append(copy)
    for copy in stores:
        copy.wait()


def body(visits, strips, images, mask_bits, visit_weight, intersection, patch_owner):
    _, pieces, rows, cols = images.shape
    blocks = rows // TILE
    distinct = max(1, patch_owner.shape[0] // 2)
    span = pieces * TILE
    taps = kernel_taps()
    collect = gather_matrix()
    width = max(collect.shape[1], cols, rows + 2 * TILE)
    width = -(-width // 128) * 128
    tables = jnp.asarray(np.concatenate([
        np.pad(part, ((0, 0), (0, width - part.shape[1])))
        for part in (
            np.transpose(band_matrix(taps, cols, cols, HALF), (0, 2, 1)).reshape(3 * cols, cols),
            band_matrix(taps, rows, rows + 2 * TILE, HALF - TILE).reshape(3 * rows, -1),
            collect,
        )
    ]), BF16)
    hbm = pl.BlockSpec(memory_space=pltpu.HBM)
    vmem = pl.BlockSpec(memory_space=pltpu.VMEM)
    smem = pl.BlockSpec(memory_space=pltpu.SMEM)
    dma = pltpu.SemaphoreType.DMA
    cross = intersection.reshape(1, pieces)
    middle = pl.pallas_call(
        functools.partial(kernel, visits, strips, distinct),
        out_shape=(
            jax.ShapeDtypeStruct((rows, cols), BF16),
            jax.ShapeDtypeStruct((blocks, pieces, TILE, cols), BF16),
            jax.ShapeDtypeStruct((distinct, BASES * TILE, blocks * cols), BF16),
            jax.ShapeDtypeStruct((distinct, span, 2 * BASES * TILE), BF16),
        ),
        in_specs=[hbm, hbm, vmem, vmem, smem, smem, hbm],
        out_specs=(vmem, vmem, vmem, vmem),
        scratch_shapes=[
            pltpu.VMEM((blocks, pieces, TILE, cols), jnp.int32),
            pltpu.VMEM(tables.shape, BF16),
            pltpu.VMEM((span, blocks * cols), BF16),
            pltpu.VMEM((span, blocks * cols), BF16),
            pltpu.VMEM((blocks, distinct, 2, TILE, cols), BF16),
            pltpu.VMEM((visits, distinct, 2, TILE, cols), BF16),
            pltpu.VMEM((1, 128), F32),
            pltpu.VMEM((visits, 1, 128), F32),
            pltpu.VMEM((blocks + 2, visits, TILE, cols), BF16),
            pltpu.VMEM((distinct, len(pairs) * TILE, blocks * cols), BF16),
            pltpu.VMEM((BASES * 8, 128), F32),
            pltpu.VMEM((max(1, strips - 1), BASES * 8, 128), F32),
            dma((2, blocks)),
            dma,
            dma((blocks,)),
            dma((visits,)),
            dma((blocks,)),
            dma((visits,)),
            dma((visits,)),
            dma((blocks,)),
            dma((2,)),
            dma((2,)),
            dma((max(1, strips - 1),)),
            dma((max(1, strips - 1),)),
        ],
        compiler_params=pltpu.CompilerParams(
            collective_id=0, has_side_effects=True, vmem_limit_bytes=55_100_000
        ),
        name="coadd_solve",
    )(
        images, mask_bits, visit_weight, cross, patch_owner, cross,
        tables,
    )
    return pl.pallas_call(
        finish,
        out_shape=(
            jax.ShapeDtypeStruct((1, 1, rows, cols), BF16),
            jax.ShapeDtypeStruct(images.shape, BF16),
        ),
        in_specs=[vmem, vmem, vmem, vmem],
        out_specs=(hbm, hbm),
        scratch_shapes=[
            pltpu.VMEM((blocks, pieces, TILE, cols), BF16),
            dma((1 + blocks,)),
        ],
        compiler_params=pltpu.CompilerParams(vmem_limit_bytes=40 * 1024 * 1024),
        name="difference",
    )(*middle)


def solution(mesh):
    in_specs = (
        P("band", ("groups", "visit"), "strip", None),
        P("band", ("groups", "visit"), "strip", None),
        P("band", ("groups", "visit")),
        P(("groups", "visit"), None),
        P("groups"),
    )
    out_specs = (
        P("band", ("groups", "visit"), "strip", None),
        P("band", ("groups", "visit"), "strip", None),
    )
    step = functools.partial(body, mesh.shape["visit"], mesh.shape["strip"])
    return jax.shard_map(step, mesh=mesh, in_specs=in_specs, out_specs=out_specs, check_vma=False)
```

profile of v0, /device:TPU:0, one launch (start us, length us, event | category | flops | bytes accessed | tf_op | source)
XLA Modules:
  0.0 24.6 jit_solution(2270854058571771100)
XLA Ops:
  0.6 0.0 copy-start.2
  0.6 0.0 copy-start
  0.7 0.0 copy-start.1
  0.7 0.6 %copy-done.2 = s32[4]{0:T(128)S(1)} copy-done((s32[4]{0:T(128)S(1)}, s32[4]{0:T(128)}, u32[]{:S(2)}) %copy-start.2) | copy-done | bytes 40
  1.3 0.0 copy-done
  1.3 0.0 copy-done.1
  1.3 22.1 %coadd_solve.1 = (bf16[64,256]{1,0:T(8,128)(2,1)S(1)}, bf16[4,16,16,256]{3,2,1,0:T(8,128)(2,1)S(1)}, bf16[2,96,1024]{2,1,0:T(8,128)(2,1)S(1)}, bf16[2,256,192]{2,1,0:T(8,128)(2,1)S(1)}) custom-call(bf16[1,16,64,256]{3,2,1,0:T(8,128)(2,1)} %images.1, s32[1,16,64,256]{3,2,1,0:T(8,128)} %masks.1, bf16[1,16]{1,0:T(2,128)(2,1)S(1)} %copy-done.1, ...), custom_call_target="tpu_custom_call" | custom-call | tf_op jit(solution)/shard_map/coadd_solve/pallas_call | solution.py:423
  23.4 1.2 %difference.1 = (bf16[1,1,64,256]{3,2,1,0:T(8,128)(2,1)}, bf16[1,16,64,256]{3,2,1,0:T(8,128)(2,1)}) custom-call(bf16[64,256]{1,0:T(8,128)(2,1)S(1)} %get-tuple-element.6.coadd_in, bf16[4,16,16,256]{3,2,1,0:T(8,128)(2,1)S(1)} %get-tuple-element.7.image_v, bf16[2,96,1024]{2,1,0:T(8,128)(2,1)S(1)} %get-tuple-element.8.basis, ...), custom_call_target="tpu_custom_call" | custom-call | tf_op jit(solution)/shard_map/difference/pallas_call | solution.py:467
Async XLA Ops:
  0.6 0.7 %copy-start.2 = (s32[4]{0:T(128)S(1)}, s32[4]{0:T(128)}, u32[]{:S(2)}) copy-start(s32[4]{0:T(128)} %owner.1) | copy-start | bytes 52
  0.6 0.7 %copy-start = (s32[16,1]{0,1:T(1,128)S(1)}, s32[16,1]{0,1:T(1,128)}, u32[]{:S(2)}) copy-start(s32[16,1]{0,1:T(1,128)} %param.9) | copy-start | bytes 196
  0.7 0.7 %copy-start.1 = (bf16[1,16]{1,0:T(2,128)(2,1)S(1)}, bf16[1,16]{1,0:T(2,128)(2,1)}, u32[]{:S(2)}) copy-start(bf16[1,16]{1,0:T(2,128)(2,1)} %weight.1) | copy-start | bytes 100
where the time goes:
time: 24.8 us; the launch traced here: 24.6 us
  Pallas kernels  23.3 us (94%)
  local copies, waits for them, and re-layouts  0.66 us (3%)
  between operations  0.66 us (3%)
    pallas_call x1, Pallas kernels, body(): pl.pallas_call(functools.partial(kernel, visits, strips, distinct), out_s...  22.1 us
    pallas_call x1, Pallas kernels, body(): pl.pallas_call(finish, out_shape=(jax.ShapeDtypeStruct((1, 1, rows, cols)...  1.18 us
    unnamed x6, local copies, waits for them, and re-layouts  0.66 us

commit v1 on v0

v1 whole, which is shorter than its diff:
```python
import functools

import jax
import jax.numpy as jnp
import numpy as np
from jax import lax
from jax.experimental import pallas as pl
from jax.experimental.pallas import tpu as pltpu
from jax.sharding import PartitionSpec as P

BASES = 6
HALF = 9
TILE = 16
LANES = 128

basis_rows = (0, 0, 1, 0, 2, 1)
basis_cols = (0, 1, 0, 2, 0, 1)
pairs = tuple((a, c) for a in range(BASES) for c in range(a, BASES))
MESH = pl.DeviceIdType.MESH
F32 = jnp.float32
BF16 = jnp.bfloat16


def kernel_taps():
    offsets = np.arange(2 * HALF + 1).astype(np.float32) - HALF
    gaussian = np.exp(-offsets * offsets / np.float32(18.0))
    centre = np.sum(offsets * offsets * gaussian * gaussian) / np.sum(gaussian * gaussian)
    table = np.stack([gaussian, offsets * gaussian, (offsets * offsets - centre) * gaussian])
    table = table / np.sqrt(np.sum(table * table, axis=1, keepdims=True))
    return table.astype(BF16).astype(np.float32)


def band_matrix(table, lead, trail, displace):
    index = np.arange(trail)[None, :] - np.arange(lead)[:, None] + displace
    inside = (index >= 0) & (index <= 2 * HALF)
    return np.where(inside[None], table[:, np.clip(index, 0, 2 * HALF)], 0.0)


def gather_matrix():
    result = np.zeros(((len(pairs) + BASES) * TILE, LANES), np.float32)
    for n, (a, c) in enumerate(pairs):
        result[n * TILE : (n + 1) * TILE, a * 8 + c] = 1.0
        result[n * TILE : (n + 1) * TILE, c * 8 + a] = 1.0
    for a in range(BASES):
        n = len(pairs) + a
        result[n * TILE : (n + 1) * TILE, a * 8 + 6] = 1.0
    return result


def iota(shape, dim):
    return lax.broadcasted_iota(jnp.int32, shape, dim)


def nn(a, b):
    return jnp.dot(a, b, preferred_element_type=F32)


def nt(a, b):
    return lax.dot_general(a, b, (((1,), (1,)), ((), ())), preferred_element_type=F32)


def tn(a, b):
    return lax.dot_general(a, b, (((0,), (0,)), ((), ())), preferred_element_type=F32)


def each(count, step):
    if count <= 4:
        for k in range(count):
            step(k)
    else:
        def body(k, carry):
            step(k)
            return carry

        lax.fori_loop(0, count, body, 0)


def thirds(value):
    high = value.astype(BF16)
    rest = value - high.astype(F32)
    middle = rest.astype(BF16)
    low = (rest - middle.astype(F32)).astype(BF16)
    return jnp.concatenate([high, middle, low], axis=0)


def kernel(
    visits, strips, distinct,
    images, masks, weight_in, cross_in, owner_in, table_in,
    coadd_out, image_v, basis, mixers,
    mask_v, tables, weight, cross, cross_scalar, owner, use, use_image, send, recv, ids_own, ids,
    patches, chosen, template_v, owned, prods, small, small_in,
    in_sem, const_sem, first_sem, rs_send, rs_recv, id_send, id_recv, ag_send, ag_recv,
    halo_send, halo_recv, own_send, own_recv, st_send, st_recv,
):
    pieces, rows, cols = images.shape[1:]
    blocks = rows // TILE
    span = pieces * TILE
    halves = cols // LANES
    lead = (visits - halves) // 2
    me = lax.axis_index("visit")
    strip = lax.axis_index("strip")
    above = strip > 0
    below = strip < strips - 1

    firsts = [
        pltpu.make_async_copy(cross_in, cross_scalar, first_sem.at[0]),
        pltpu.make_async_copy(owner_in, owner, first_sem.at[1]),
        pltpu.make_async_copy(cross_in, cross, first_sem.at[2]),
        pltpu.make_async_copy(weight_in, weight, first_sem.at[3]),
    ]
    for copy in firsts:
        copy.start()

    barrier = pltpu.get_barrier_semaphore()
    for k in range(visits):
        for hop in range(strips):
            if k == 0 and hop == 0:
                continue
            target = {"visit": lax.rem(me + k, visits), "strip": lax.rem(strip + hop, strips)}
            pl.semaphore_signal(barrier, inc=1, device_id=target, device_id_type=MESH)

    loads = []
    for t in range(blocks):
        piece_rows = pl.ds(t * TILE, TILE)
        loads.append((
            pltpu.make_async_copy(masks.at[0, :, piece_rows, :], mask_v.at[t], in_sem.at[0, t]),
            pltpu.make_async_copy(images.at[0, :, piece_rows, :], image_v.at[t], in_sem.at[1, t]),
        ))
        for copy in loads[t]:
            copy.start()
    constants = pltpu.make_async_copy(table_in, tables, const_sem)
    constants.start()

    for copy in firsts:
        copy.wait()
    seats = [owner[cross_scalar[0, j]] for j in range(pieces)]
    slots = [jnp.int32(0)] * distinct
    rank = jnp.int32(0)
    for q in range(visits):
        present = jnp.int32(0)
        for j in range(pieces):
            present = present | jnp.where(seats[j] == q, 1, 0)
        for d in range(distinct):
            slots[d] = slots[d] + jnp.where((present == 1) & (rank == d), q, 0)
        rank = rank + present

    position = jnp.zeros((1, pieces), jnp.int32)
    for p in range(visits):
        position = position + jnp.where(cross[...] == p, owner[p], 0)
    e2 = iota((pieces, span), 0) == jnp.right_shift(iota((pieces, span), 1), 4)
    e2 = e2.astype(F32).astype(BF16)
    pair = jnp.where(
        iota((8, pieces), 0) == 0, weight[...].astype(F32), position.astype(F32)
    ).astype(BF16)
    wide = nn(pair, e2)
    same = (iota((TILE, span), 0) & (TILE - 1)) == (iota((TILE, span), 1) & (TILE - 1))
    adder = jnp.concatenate([
        jnp.where(same & (wide[1:2] == lax.convert_element_type(slots[d], F32)), wide[0:1], 0.0)
        for d in range(distinct)
    ], axis=0).astype(BF16)

    for t in range(blocks):
        for copy in loads[t]:
            copy.wait()
        usable = ((mask_v[t].reshape(span, cols) & 3) != 3).astype(F32).astype(BF16)
        masked = usable * image_v[t].reshape(span, cols)
        lanes = pl.ds(t * cols, cols)
        use[:, lanes] = usable
        use_image[:, lanes] = masked
        for part, value in enumerate((masked, usable)):
            total = nn(adder, value).astype(BF16)
            for d in range(distinct):
                for h in range(halves):
                    send[h, d, part, pl.ds(t * TILE, TILE), :] = total[
                        d * TILE : (d + 1) * TILE, h * LANES : (h + 1) * LANES
                    ]
    names = jnp.zeros((1, LANES), jnp.int32)
    for d in range(distinct):
        names = names + jnp.where(iota((1, LANES), 1) == d, slots[d], 0)
    ids_own[...] = names.astype(F32)

    def sum_copies(h, source):
        return (
            pltpu.make_async_remote_copy(
                src_ref=ids_own, dst_ref=ids.at[source],
                send_sem=id_send.at[h], recv_sem=id_recv.at[source],
                device_id={"visit": lead + h}, device_id_type=MESH,
            ),
            pltpu.make_async_remote_copy(
                src_ref=send.at[h], dst_ref=recv.at[source],
                send_sem=rs_send.at[h], recv_sem=rs_recv.at[source],
                device_id={"visit": lead + h}, device_id_type=MESH,
            ),
        )

    def template_copy(h, v, d):
        return pltpu.make_async_remote_copy(
            src_ref=chosen.at[v, d], dst_ref=template_v.at[d, h, pl.ds(TILE, rows), :],
            send_sem=ag_send.at[v, d], recv_sem=ag_recv.at[h, d],
            device_id={"visit": v}, device_id_type=MESH,
        )

    def edge_copy(way, h, v, d):
        step, source, target = ((1, rows - TILE, 0), (strips - 1, 0, rows + TILE))[way]
        return pltpu.make_async_remote_copy(
            src_ref=chosen.at[v, d, pl.ds(source, TILE), :],
            dst_ref=template_v.at[d, h, pl.ds(target, TILE), :],
            send_sem=halo_send.at[way, v, d], recv_sem=halo_recv.at[way, h, d],
            device_id={"visit": v, "strip": lax.rem(strip + step, strips)}, device_id_type=MESH,
        )

    def owned_copy(h, v):
        return pltpu.make_async_remote_copy(
            src_ref=patches.at[v], dst_ref=owned.at[h],
            send_sem=own_send.at[v], recv_sem=own_recv.at[h],
            device_id={"visit": v}, device_id_type=MESH,
        )

    pl.semaphore_wait(barrier, visits * strips - 1)
    for h in range(halves):
        @pl.when(me != lead + h)
        def _():
            for copy in sum_copies(h, me):
                copy.start()

    @pl.when(jnp.logical_not(above))
    def _():
        template_v[:, :, pl.ds(0, TILE), :] = jnp.zeros((distinct, halves, TILE, LANES), BF16)

    @pl.when(jnp.logical_not(below))
    def _():
        template_v[:, :, pl.ds(rows + TILE, TILE), :] = jnp.zeros(
            (distinct, halves, TILE, LANES), BF16
        )

    mine = me - lead
    owning = (me >= lead) & (me < lead + halves)

    def id_tile(v, d):
        return jnp.broadcast_to(ids[v][:, d : d + 1], (TILE, LANES))

    def reduce():
        recv[me] = send[mine]
        ids[me] = ids_own[...]
        for v in range(visits):
            @pl.when(me != v)
            def _():
                for copy in sum_copies(0, v):
                    copy.wait_recv()

        def one_tile(t):
            piece_rows = pl.ds(t * TILE, TILE)
            if visits <= 4:
                tiles = [[id_tile(v, d) for d in range(distinct)] for v in range(visits)]
                finals = []
                for q in range(visits):
                    numerator = jnp.zeros((TILE, LANES), F32)
                    denominator = jnp.zeros((TILE, LANES), F32)
                    for v in range(visits):
                        for d in range(distinct):
                            here = tiles[v][d] == float(q)
                            numerator += jnp.where(
                                here, recv[v, d, 0, piece_rows, :].astype(F32), 0.0
                            )
                            denominator += jnp.where(
                                here, recv[v, d, 1, piece_rows, :].astype(F32), 0.0
                            )
                    final = numerator / jnp.maximum(denominator, 1.0)
                    patches[q, piece_rows, :] = final.astype(BF16)
                    finals.append(final)
                for v in range(visits):
                    for d in range(distinct):
                        picked = finals[0]
                        for q in range(1, visits):
                            picked = jnp.where(tiles[v][d] == float(q), finals[q], picked)
                        chosen[v, d, piece_rows, :] = picked.astype(BF16)
                return

            def one_patch(q):
                number = lax.convert_element_type(q, F32)

                def add(v, carry):
                    numerator, denominator = carry
                    for d in range(distinct):
                        here = id_tile(v, d) == number
                        numerator += jnp.where(here, recv[v, d, 0, piece_rows, :].astype(F32), 0.0)
                        denominator += jnp.where(here, recv[v, d, 1, piece_rows, :].astype(F32), 0.0)
                    return numerator, denominator

                zero = jnp.zeros((TILE, LANES), F32)
                numerator, denominator = lax.fori_loop(0, visits, add, (zero, zero))
                final = numerator / jnp.maximum(denominator, 1.0)
                patches[q, piece_rows, :] = final.astype(BF16)

            def pick(v):
                for d in range(distinct):
                    tile = id_tile(v, d)

                    def better(q, picked):
                        final = patches[q, piece_rows, :].astype(F32)
                        return jnp.where(tile == lax.convert_element_type(q, F32), final, picked)

                    picked = lax.fori_loop(0, visits, better, jnp.zeros((TILE, LANES), F32))
                    chosen[v, d, piece_rows, :] = picked.astype(BF16)

            each(visits, one_patch)
            each(visits, pick)

        for t in range(blocks):
            one_tile(t)

        for d in range(distinct):
            def templates(v):
                pl.when(below)(edge_copy(0, mine, v, d).start)
                pl.when(above)(edge_copy(1, mine, v, d).start)

                @pl.when(me != v)
                def _():
                    template_copy(mine, v, d).start()

            each(visits, templates)

        def owners(v):
            @pl.when(me != v)
            def _():
                owned_copy(mine, v).start()

        each(visits, owners)
        template_v[:, mine, pl.ds(TILE, rows), :] = chosen[me]
        owned[mine] = patches[me]

    pl.when(owning)(reduce)
    constants.wait()

    across_top, up_top = 0, BASES // 2 * cols
    gather_top = up_top + 3 * rows
    vertical = tables[pl.ds(up_top, 3 * rows), pl.ds(0, rows + 2 * TILE)]

    def across(c):
        return tables[pl.ds(across_top + c * cols, cols), pl.ds(0, cols)]

    one_hot = (position == iota((LANES, pieces), 0)).astype(F32).astype(BF16)
    e_rows = jnp.right_shift(iota((span, LANES), 0), 4) == iota((span, LANES), 1)
    e_rows = e_rows.astype(F32).astype(BF16)
    row_hot = nt(e_rows[:, :pieces], one_hot)
    piece_hot = nt((iota((TILE, pieces), 0) == iota((TILE, pieces), 1)).astype(F32).astype(BF16), one_hot)

    def member(d, hot):
        chosen_one = jnp.where(iota(hot.shape, 1) == slots[d], hot, 0.0)
        return jnp.sum(chosen_one, axis=1, keepdims=True)

    def summed(values):
        return jnp.sum(values.reshape(pieces, TILE, values.shape[1]), axis=1)

    def keep(width):
        return (iota((span, width), 0) & (TILE - 1)) == (iota((span, width), 1) & (TILE - 1))

    wide_n = len(pairs) * TILE
    wide_b = BASES * TILE
    normal = jnp.zeros((pieces, wide_n), F32)
    right = jnp.zeros((pieces, wide_b), F32)
    for d in range(distinct):
        for h in range(halves):
            @pl.when(me != lead + h)
            def _():
                template_copy(h, me, d).wait_recv()

            pl.when(above)(edge_copy(0, h, me, d).wait_recv)
            pl.when(below)(edge_copy(1, h, me, d).wait_recv)
        template = jnp.concatenate([template_v[d, h] for h in range(halves)], axis=1)
        smooth = nn(vertical, template).astype(BF16)
        planes = [None] * BASES
        for c in range(3):
            taken = [a for a in range(BASES) if basis_cols[a] == c]
            product = nn(smooth[: len(taken) * rows], across(c)).astype(BF16)
            for a in taken:
                r = basis_rows[a]
                planes[a] = product[r * rows : (r + 1) * rows]
        for a in range(BASES):
            for t in range(blocks):
                basis[d, pl.ds(a * TILE, TILE), pl.ds(t * cols, cols)] = planes[a][
                    t * TILE : (t + 1) * TILE
                ]
        for n, (a, c) in enumerate(pairs):
            product = planes[a] * planes[c]
            for t in range(blocks):
                prods[d, pl.ds(n * TILE, TILE), pl.ds(t * cols, cols)] = product[
                    t * TILE : (t + 1) * TILE
                ]
        belongs = member(d, row_hot)
        normal = normal + summed(jnp.where(keep(wide_n), nt(use[...], prods[d]), 0.0) * belongs)
        right = right + summed(jnp.where(keep(wide_b), nt(use_image[...], basis[d]), 0.0) * belongs)

    gather_n = tables[pl.ds(gather_top, wide_n), pl.ds(0, LANES)]
    gather_b = tables[pl.ds(gather_top + wide_n, wide_b), pl.ds(0, LANES)]
    system = nn(thirds(normal), gather_n) + nn(thirds(right), gather_b)
    small[...] = sum(system[k * pieces : (k + 1) * pieces] for k in range(3))
    exchanges = []
    for hop in range(1, strips):
        exchanges.append(pltpu.make_async_remote_copy(
            src_ref=small, dst_ref=small_in.at[hop - 1],
            send_sem=st_send.at[hop - 1], recv_sem=st_recv.at[hop - 1],
            device_id={"strip": lax.rem(strip + hop, strips)}, device_id_type=MESH,
        ))
    for copy in exchanges:
        copy.start()

    wide_c = 2 * wide_b
    column = iota((16, wide_c), 1)
    source = jnp.where(
        column < wide_b, jnp.right_shift(column, 4), jnp.right_shift(column - wide_b, 4) + 8
    )
    e3 = (source == iota((16, wide_c), 0)).astype(F32).astype(BF16)
    diagonal = iota((TILE, wide_c), 0) == (iota((TILE, wide_c), 1) & (TILE - 1))
    belongs = [member(d, piece_hot) for d in range(distinct)]

    for h in range(halves):
        @pl.when(me != lead + h)
        def _():
            owned_copy(h, me).wait_recv()

        coadd_out[:, pl.ds(h * LANES, LANES)] = owned[h]

    full = small[...]
    for hop in range(1, strips):
        exchanges[hop - 1].wait_recv()
        full = full + small_in[hop - 1]
    full = jnp.transpose(full)

    line = iota((8, pieces), 0)
    table = [
        full[a * 8 : (a + 1) * 8] + jnp.where(line == a, 1.0, 0.0) for a in range(BASES)
    ]
    for column in range(BASES):
        pivot = table[column] / table[column][column : column + 1]
        for i in range(BASES):
            if i != column:
                table[i] = table[i] - table[i][column : column + 1] * pivot
        table[column] = pivot
    found = jnp.zeros((8, pieces), F32)
    for a in range(BASES):
        found = found + jnp.where(line == a, table[a][BASES : BASES + 1], 0.0)
    high = found.astype(BF16).astype(F32)
    low = found - high
    both = jnp.concatenate([high, low], axis=0).astype(BF16)
    spread = tn(both, e3)
    for d in range(distinct):
        part = spread * belongs[d]
        for j in range(pieces):
            mixers[d, pl.ds(j * TILE, TILE), :] = jnp.where(
                diagonal, part[j : j + 1], 0.0
            ).astype(BF16)

    for copy in exchanges:
        copy.wait_send()
    for h in range(halves):
        @pl.when(me != lead + h)
        def _():
            for copy in sum_copies(h, me):
                copy.wait_send()

    @pl.when(owning)
    def _():
        def sent(v):
            for d in range(distinct):
                pl.when(below)(edge_copy(0, mine, v, d).wait_send)
                pl.when(above)(edge_copy(1, mine, v, d).wait_send)

            @pl.when(me != v)
            def _():
                for d in range(distinct):
                    template_copy(mine, v, d).wait_send()
                owned_copy(mine, v).wait_send()

        each(visits, sent)


def finish(coadd_in, image_v, basis, mixers, coadd_out, diff_out, diff_v, out_sem):
    distinct = basis.shape[0]
    blocks, pieces, _, cols = image_v.shape
    span = pieces * TILE
    stores = [pltpu.make_async_copy(coadd_in, coadd_out.at[0, 0], out_sem.at[0])]
    stores[0].start()
    for t in range(blocks):
        lanes = pl.ds(t * cols, cols)
        fitted = jnp.zeros((span, cols), F32)
        for d in range(distinct):
            planes = basis[d, :, lanes]
            fitted = fitted + nn(mixers[d], jnp.concatenate([planes, planes], axis=0))
        result = (image_v[t].reshape(span, cols).astype(F32) - fitted).astype(BF16)
        diff_v[t] = result.reshape(pieces, TILE, cols)
        copy = pltpu.make_async_copy(
            diff_v.at[t], diff_out.at[0, :, pl.ds(t * TILE, TILE), :], out_sem.at[1 + t]
        )
        copy.start()
        stores.append(copy)
    for copy in stores:
        copy.wait()


def body(visits, strips, images, mask_bits, visit_weight, intersection, patch_owner):
    _, pieces, rows, cols = images.shape
    blocks = rows // TILE
    halves = cols // LANES
    distinct = max(1, patch_owner.shape[0] // 2)
    span = pieces * TILE
    taps = kernel_taps()
    width = -(-max(LANES, cols, rows + 2 * TILE) // LANES) * LANES
    tables = jnp.asarray(np.concatenate([
        np.pad(part, ((0, 0), (0, width - part.shape[1])))
        for part in (
            np.transpose(band_matrix(taps, cols, cols, HALF), (0, 2, 1)).reshape(3 * cols, cols),
            band_matrix(taps, rows, rows + 2 * TILE, HALF - TILE).reshape(3 * rows, -1),
            gather_matrix(),
        )
    ]), BF16)
    hbm = pl.BlockSpec(memory_space=pltpu.HBM)
    vmem = pl.BlockSpec(memory_space=pltpu.VMEM)
    dma = pltpu.SemaphoreType.DMA
    cross = intersection.reshape(1, pieces)
    others = max(1, strips - 1)
    middle = pl.pallas_call(
        functools.partial(kernel, visits, strips, distinct),
        out_shape=(
            jax.ShapeDtypeStruct((rows, cols), BF16),
            jax.ShapeDtypeStruct((blocks, pieces, TILE, cols), BF16),
            jax.ShapeDtypeStruct((distinct, BASES * TILE, blocks * cols), BF16),
            jax.ShapeDtypeStruct((distinct, span, 2 * BASES * TILE), BF16),
        ),
        in_specs=[hbm, hbm, hbm, hbm, hbm, hbm],
        out_specs=(vmem, vmem, vmem, vmem),
        scratch_shapes=[
            pltpu.VMEM((blocks, pieces, TILE, cols), jnp.int32),
            pltpu.VMEM(tables.shape, BF16),
            pltpu.VMEM((1, pieces), BF16),
            pltpu.VMEM((1, pieces), jnp.int32),
            pltpu.SMEM((1, pieces), jnp.int32),
            pltpu.SMEM(patch_owner.shape, jnp.int32),
            pltpu.VMEM((span, blocks * cols), BF16),
            pltpu.VMEM((span, blocks * cols), BF16),
            pltpu.VMEM((halves, distinct, 2, rows, LANES), BF16),
            pltpu.VMEM((visits, distinct, 2, rows, LANES), BF16),
            pltpu.VMEM((1, LANES), F32),
            pltpu.VMEM((visits, 1, LANES), F32),
            pltpu.VMEM((visits, rows, LANES), BF16),
            pltpu.VMEM((visits, distinct, rows, LANES), BF16),
            pltpu.VMEM((distinct, halves, rows + 2 * TILE, LANES), BF16),
            pltpu.VMEM((halves, rows, LANES), BF16),
            pltpu.VMEM((distinct, len(pairs) * TILE, blocks * cols), BF16),
            pltpu.VMEM((pieces, LANES), F32),
            pltpu.VMEM((others, pieces, LANES), F32),
            dma((2, blocks)),
            dma,
            dma((4,)),
            dma((halves,)),
            dma((visits,)),
            dma((halves,)),
            dma((visits,)),
            dma((visits, distinct)),
            dma((halves, distinct)),
            dma((2, visits, distinct)),
            dma((2, halves, distinct)),
            dma((visits,)),
            dma((halves,)),
            dma((others,)),
            dma((others,)),
        ],
        compiler_params=pltpu.CompilerParams(
            collective_id=0, has_side_effects=True, vmem_limit_bytes=55_100_000
        ),
        name="coadd_solve",
    )(images, mask_bits, visit_weight, cross, patch_owner, tables)
    return pl.pallas_call(
        finish,
        out_shape=(
            jax.ShapeDtypeStruct((1, 1, rows, cols), BF16),
            jax.ShapeDtypeStruct(images.shape, BF16),
        ),
        in_specs=[vmem, vmem, vmem, vmem],
        out_specs=(hbm, hbm),
        scratch_shapes=[
            pltpu.VMEM((blocks, pieces, TILE, cols), BF16),
            dma((1 + blocks,)),
        ],
        compiler_params=pltpu.CompilerParams(vmem_limit_bytes=40 * 1024 * 1024),
        name="difference",
    )(*middle)


def solution(mesh):
    in_specs = (
        P("band", ("groups", "visit"), "strip", None),
        P("band", ("groups", "visit"), "strip", None),
        P("band", ("groups", "visit")),
        P(("groups", "visit"), None),
        P("groups"),
    )
    out_specs = (
        P("band", ("groups", "visit"), "strip", None),
        P("band", ("groups", "visit"), "strip", None),
    )
    step = functools.partial(body, mesh.shape["visit"], mesh.shape["strip"])
    return jax.shard_map(step, mesh=mesh, in_specs=in_specs, out_specs=out_specs, check_vma=False)
```

time: 24.8 us -> 23.2 us (0.935)
  Pallas kernels: 23.3 us -> 21.7 us
    pallas_call x1, Pallas kernels: 22.1 us -> 20.5 us  [body(): pl.pallas_call(functools.partial(kernel, visits, strips, distinct), out_s...]
where the time goes in v1:
time: 23.2 us; the launch traced here: 23 us
  Pallas kernels  21.7 us (94%)
  local copies, waits for them, and re-layouts  0.66 us (3%)
  between operations  0.66 us (3%)
    pallas_call x1, Pallas kernels, body(): pl.pallas_call(functools.partial(kernel, visits, strips, distinct), out_s...  20.5 us
    pallas_call x1, Pallas kernels, body(): pl.pallas_call(finish, out_shape=(jax.ShapeDtypeStruct((1, 1, rows, cols)...  1.18 us
    unnamed x6, local copies, waits for them, and re-layouts  0.66 us

profile of v1, /device:TPU:0, one launch (start us, length us, event | category | flops | bytes accessed | tf_op | source)
XLA Modules:
  0.0 23.0 jit_solution(12576906372796379577)
XLA Ops:
  0.6 0.0 copy-start.2
  0.6 0.0 copy-start.1
  0.7 0.0 copy-start
  0.7 0.6 %copy-done.2 = s32[4]{0:T(128)S(1)} copy-done((s32[4]{0:T(128)S(1)}, s32[4]{0:T(128)}, u32[]{:S(2)}) %copy-start.2) | copy-done | bytes 40
  1.3 0.0 copy-done.1
  1.3 0.0 copy-done
  1.3 20.5 %coadd_solve.1 = (bf16[64,256]{1,0:T(8,128)(2,1)S(1)}, bf16[4,16,16,256]{3,2,1,0:T(8,128)(2,1)S(1)}, bf16[2,96,1024]{2,1,0:T(8,128)(2,1)S(1)}, bf16[2,256,192]{2,1,0:T(8,128)(2,1)S(1)}) custom-call(bf16[1,16,64,256]{3,2,1,0:T(8,128)(2,1)} %images.1, s32[1,16,64,256]{3,2,1,0:T(8,128)} %masks.1, bf16[1,16]{1,0:T(2,128)(2,1)S(1)} %copy-done, ...), custom_call_target="tpu_custom_call" | custom-call | tf_op jit(solution)/shard_map/coadd_solve/pallas_call | solution.py:522
  21.9 1.2 %difference.1 = (bf16[1,1,64,256]{3,2,1,0:T(8,128)(2,1)}, bf16[1,16,64,256]{3,2,1,0:T(8,128)(2,1)}) custom-call(bf16[64,256]{1,0:T(8,128)(2,1)S(1)} %get-tuple-element.6.coadd_in, bf16[4,16,16,256]{3,2,1,0:T(8,128)(2,1)S(1)} %get-tuple-element.7.image_v, bf16[2,96,1024]{2,1,0:T(8,128)(2,1)S(1)} %get-tuple-element.8.basis, ...), custom_call_target="tpu_custom_call" | custom-call | tf_op jit(solution)/shard_map/difference/pallas_call | solution.py:573
Async XLA Ops:
  0.6 0.7 %copy-start.2 = (s32[4]{0:T(128)S(1)}, s32[4]{0:T(128)}, u32[]{:S(2)}) copy-start(s32[4]{0:T(128)} %owner_in.1) | copy-start | bytes 52
  0.6 0.7 %copy-start.1 = (s32[16,1]{0,1:T(1,128)S(1)}, s32[16,1]{0,1:T(1,128)}, u32[]{:S(2)}) copy-start(s32[16,1]{0,1:T(1,128)} %param.9) | copy-start | bytes 196
  0.7 0.7 %copy-start = (bf16[1,16]{1,0:T(2,128)(2,1)S(1)}, bf16[1,16]{1,0:T(2,128)(2,1)}, u32[]{:S(2)}) copy-start(bf16[1,16]{1,0:T(2,128)(2,1)} %weight_in.1) | copy-start | bytes 100

commit v2 on v1

v2 whole, which is shorter than its diff:
```python
import functools

import jax
import jax.numpy as jnp
import numpy as np
from jax import lax
from jax.experimental import pallas as pl
from jax.experimental.pallas import tpu as pltpu
from jax.sharding import PartitionSpec as P

BASES = 6
HALF = 9
TILE = 16
LANES = 128

basis_rows = (0, 0, 1, 0, 2, 1)
basis_cols = (0, 1, 0, 2, 0, 1)
pairs = tuple((a, c) for a in range(BASES) for c in range(a, BASES))
MESH = pl.DeviceIdType.MESH
F32 = jnp.float32
BF16 = jnp.bfloat16


def kernel_taps():
    offsets = np.arange(2 * HALF + 1).astype(np.float32) - HALF
    gaussian = np.exp(-offsets * offsets / np.float32(18.0))
    centre = np.sum(offsets * offsets * gaussian * gaussian) / np.sum(gaussian * gaussian)
    table = np.stack([gaussian, offsets * gaussian, (offsets * offsets - centre) * gaussian])
    table = table / np.sqrt(np.sum(table * table, axis=1, keepdims=True))
    return table.astype(BF16).astype(np.float32)


def band_matrix(table, lead, trail, displace):
    index = np.arange(trail)[None, :] - np.arange(lead)[:, None] + displace
    inside = (index >= 0) & (index <= 2 * HALF)
    return np.where(inside[None], table[:, np.clip(index, 0, 2 * HALF)], 0.0)


def iota(shape, dim):
    return lax.broadcasted_iota(jnp.int32, shape, dim)


def nn(a, b):
    return jnp.dot(a, b, preferred_element_type=F32)


def nt(a, b):
    return lax.dot_general(a, b, (((1,), (1,)), ((), ())), preferred_element_type=F32)


def tn(a, b):
    return lax.dot_general(a, b, (((0,), (0,)), ((), ())), preferred_element_type=F32)


def each(count, step):
    if count <= 4:
        for k in range(count):
            step(k)
    else:
        def body(k, carry):
            step(k)
            return carry

        lax.fori_loop(0, count, body, 0)


def thirds(value):
    high = value.astype(BF16)
    rest = value - high.astype(F32)
    middle = rest.astype(BF16)
    low = (rest - middle.astype(F32)).astype(BF16)
    return jnp.concatenate([high, middle, low], axis=0)


def kernel(
    visits, strips, bands, distinct,
    images, masks, weight_in, cross_in, owner_in, table_in,
    coadd_out, image_s, basis, mixers, order_out,
    mask_v, image_v, tables, weight, cross, owner, use, use_image, turned, turned_image, send, recv,
    patches, chosen, template_v, owned, prods, small, small_in,
    first_sem, in_sem, const_sem, sum_send, sum_recv, template_send, template_recv, owned_recv,
    st_send, st_recv,
):
    pieces, rows, cols = images.shape[1:]
    blocks = rows // TILE
    chunk = rows // in_sem.shape[1]
    span = pieces * TILE
    cap = pieces // distinct
    halves = cols // LANES
    lead = (visits - halves) // 2
    last = bands - 1
    sheet = distinct * 2 * rows
    parcel = sheet + TILE
    me = lax.axis_index("visit")
    strip = lax.axis_index("strip")
    band = lax.axis_index("band")
    above = strip > 0
    below = strip < strips - 1
    mine = me - lead
    central = (me >= lead) & (me < lead + halves)
    owning = central & (band == last)
    reach = 1 + above.astype(jnp.int32) + below.astype(jnp.int32)

    firsts = [
        pltpu.make_async_copy(cross_in, cross, first_sem.at[0]),
        pltpu.make_async_copy(owner_in, owner, first_sem.at[1]),
        pltpu.make_async_copy(weight_in, weight, first_sem.at[2]),
    ]
    for copy in firsts:
        copy.start()

    barrier = pltpu.get_barrier_semaphore()

    def greet(v, hop, b):
        target = {"visit": v, "strip": lax.rem(strip + hop, strips), "band": b}
        pl.semaphore_signal(barrier, inc=1, device_id=target, device_id_type=MESH)

    def near(hop, step):
        if hop == 0:
            step()
        elif hop == 1 and strips == 2:
            step()
        elif hop == 1:
            pl.when(below)(step)
        elif hop == strips - 1:
            pl.when(above)(step)

    def adjoining(hop):
        if hop in (0, 1) and strips == 2:
            return jnp.bool_(True)
        return below if hop == 1 else (above if hop == strips - 1 else jnp.bool_(False))

    @pl.when(owning)
    def _():
        for hop in sorted({0, 1 % strips, strips - 1}):
            def greet_strip():
                def greet_visit(v):
                    for b in range(bands):
                        if hop == 0 and b == last:
                            pl.when(me != v)(functools.partial(greet, v, hop, b))
                        else:
                            greet(v, hop, b)

                each(visits, greet_visit)

            near(hop, greet_strip)
        for hop in range(2, strips - 1):
            greet(me, hop, band)
        for hop in sorted({1 % strips, strips - 1} - {0}):
            if strips > 2:
                pl.when(jnp.logical_not(adjoining(hop)))(functools.partial(greet, me, hop, band))

    @pl.when(jnp.logical_not(owning))
    def _():
        for hop in sorted({0, 1 % strips, strips - 1}):
            def greet_owners():
                for h in range(halves):
                    greet(lead + h, hop, last)

            near(hop, greet_owners)
        for hop in range(1, strips):
            greet(me, hop, band)

    loads = []
    for k in range(rows // chunk):
        part = pl.ds(k * chunk, chunk)
        loads.append((
            pltpu.make_async_copy(masks.at[0, :, part, :], mask_v.at[:, part, :], in_sem.at[0, k]),
            pltpu.make_async_copy(images.at[0, :, part, :], image_v.at[:, part, :], in_sem.at[1, k]),
        ))
        for copy in loads[k]:
            copy.start()
    constants = pltpu.make_async_copy(table_in, tables, const_sem)
    constants.start()

    for copy in firsts:
        copy.wait()
    seats = [owner[cross[0, j]] for j in range(pieces)]
    slots = [jnp.int32(0)] * distinct
    rank = jnp.int32(0)
    for q in range(visits):
        present = jnp.int32(0)
        for j in range(pieces):
            present = present | jnp.where(seats[j] == q, 1, 0)
        for d in range(distinct):
            slots[d] = slots[d] + jnp.where((present == 1) & (rank == d), q, 0)
        rank = rank + present

    position = jnp.zeros((1, pieces), jnp.int32)
    for j in range(pieces):
        position = position + jnp.where(iota((1, pieces), 1) == j, seats[j], 0)
    e2 = iota((pieces, span), 0) == jnp.right_shift(iota((pieces, span), 1), 4)
    e2 = e2.astype(F32).astype(BF16)
    pair = jnp.where(
        iota((8, pieces), 0) == 0, weight[...].astype(F32), position.astype(F32)
    ).astype(BF16)
    wide = nn(pair, e2)
    same = (iota((TILE, span), 0) & (TILE - 1)) == (iota((TILE, span), 1) & (TILE - 1))
    adder = jnp.concatenate([
        jnp.where(same & (wide[1:2] == lax.convert_element_type(slots[d], F32)), wide[0:1], 0.0)
        for d in range(distinct)
    ], axis=0).astype(BF16)
    names = jnp.zeros((TILE, LANES), jnp.int32)
    for d in range(distinct):
        names = names + jnp.where(iota((TILE, LANES), 0) == d, slots[d], 0)
    for h in range(halves):
        send[h, pl.ds(sheet, TILE), :] = names.astype(F32).astype(BF16)

    for t in range(blocks):
        if t * TILE % chunk == 0:
            for copy in loads[t * TILE // chunk]:
                copy.wait()
        piece_rows = pl.ds(t * TILE, TILE)
        lanes = pl.ds(t * cols, cols)
        usable = ((mask_v[:, piece_rows, :].reshape(span, cols) & 3) != 3).astype(F32).astype(BF16)
        masked = usable * image_v[:, piece_rows, :].reshape(span, cols)
        use[:, :, lanes] = usable.reshape(pieces, TILE, cols)
        use_image[:, :, lanes] = masked.reshape(pieces, TILE, cols)
        for part, value in enumerate((masked, usable)):
            total = nn(adder, value).astype(BF16)
            for d in range(distinct):
                for h in range(halves):
                    send[h, pl.ds((d * 2 + part) * rows + t * TILE, TILE), :] = total[
                        d * TILE : (d + 1) * TILE, h * LANES : (h + 1) * LANES
                    ]

    def parcel_at(b, v):
        return pl.multiple_of((b * visits + v) * parcel, TILE)

    def some(count):
        return recv.at[pl.ds(0, count), :]

    def sum_copy(h, b):
        return pltpu.make_async_remote_copy(
            src_ref=send.at[h], dst_ref=recv.at[pl.ds(parcel_at(b, me), parcel), :],
            send_sem=sum_send, recv_sem=sum_recv.at[b],
            device_id={"visit": lead + h, "band": last}, device_id_type=MESH,
        )

    def template_copy(b, h, v, d):
        return pltpu.make_async_remote_copy(
            src_ref=chosen.at[b, v, d], dst_ref=template_v.at[d, h, pl.ds(TILE, rows), :],
            send_sem=template_send, recv_sem=template_recv.at[d],
            device_id={"visit": v, "band": b}, device_id_type=MESH,
        )

    def edge_copy(way, b, h, v, d):
        step, source, target = ((1, rows - TILE, 0), (strips - 1, 0, rows + TILE))[way]
        return pltpu.make_async_remote_copy(
            src_ref=chosen.at[b, v, d, pl.ds(source, TILE), :],
            dst_ref=template_v.at[d, h, pl.ds(target, TILE), :],
            send_sem=template_send, recv_sem=template_recv.at[d],
            device_id={"visit": v, "strip": lax.rem(strip + step, strips), "band": b},
            device_id_type=MESH,
        )

    def owned_copy(b, h, v):
        return pltpu.make_async_remote_copy(
            src_ref=patches.at[b, v], dst_ref=owned.at[h],
            send_sem=template_send, recv_sem=owned_recv,
            device_id={"visit": v, "band": b}, device_id_type=MESH,
        )

    def wait_for(sem, count):
        pltpu.make_async_copy(some(count), some(count), sem).wait()

    met = jnp.where(
        owning, visits * bands * reach - 1 + strips - reach, halves * reach + strips - 1
    )
    pl.semaphore_wait(barrier, met)
    for b in range(bands):
        for h in range(halves):
            @pl.when((band == b) & jnp.logical_not(owning & (mine == h)))
            def _():
                sum_copy(h, b).start()

    @pl.when(jnp.logical_not(above))
    def _():
        template_v[:, :, pl.ds(0, TILE), :] = jnp.zeros((distinct, halves, TILE, LANES), BF16)

    @pl.when(jnp.logical_not(below))
    def _():
        template_v[:, :, pl.ds(rows + TILE, TILE), :] = jnp.zeros(
            (distinct, halves, TILE, LANES), BF16
        )

    def reduce(b):
        if b == last:
            recv[pl.ds(parcel_at(b, me), parcel), :] = send[mine]
        wait_for(sum_recv.at[b], (visits if b != last else visits - 1) * parcel)

        def id_tile(v, d):
            names = recv[pl.ds(parcel_at(b, v) + sheet, TILE), :].astype(F32)
            return jnp.broadcast_to(names[d : d + 1], (TILE, LANES))

        def value(v, d, part, t):
            start = pl.multiple_of(parcel_at(b, v) + (d * 2 + part) * rows + t * TILE, TILE)
            return recv[pl.ds(start, TILE), :].astype(F32)

        def one_tile(t):
            piece_rows = pl.ds(t * TILE, TILE)
            if visits <= 4:
                tiles = [[id_tile(v, d) for d in range(distinct)] for v in range(visits)]
                finals = []
                for q in range(visits):
                    numerator = jnp.zeros((TILE, LANES), F32)
                    denominator = jnp.zeros((TILE, LANES), F32)
                    for v in range(visits):
                        for d in range(distinct):
                            here = tiles[v][d] == float(q)
                            numerator += jnp.where(here, value(v, d, 0, t), 0.0)
                            denominator += jnp.where(here, value(v, d, 1, t), 0.0)
                    final = numerator / jnp.maximum(denominator, 1.0)
                    patches[b, q, piece_rows, :] = final.astype(BF16)
                    finals.append(final)
                for v in range(visits):
                    for d in range(distinct):
                        picked = finals[0]
                        for q in range(1, visits):
                            picked = jnp.where(tiles[v][d] == float(q), finals[q], picked)
                        chosen[b, v, d, piece_rows, :] = picked.astype(BF16)
                return

            def one_patch(q):
                number = lax.convert_element_type(q, F32)

                def add(v, carry):
                    numerator, denominator = carry
                    for d in range(distinct):
                        here = id_tile(v, d) == number
                        numerator += jnp.where(here, value(v, d, 0, t), 0.0)
                        denominator += jnp.where(here, value(v, d, 1, t), 0.0)
                    return numerator, denominator

                zero = jnp.zeros((TILE, LANES), F32)
                numerator, denominator = lax.fori_loop(0, visits, add, (zero, zero))
                final = numerator / jnp.maximum(denominator, 1.0)
                patches[b, q, piece_rows, :] = final.astype(BF16)

            def pick(v):
                for d in range(distinct):
                    tile = id_tile(v, d)

                    def better(q, picked):
                        final = patches[b, q, piece_rows, :].astype(F32)
                        return jnp.where(tile == lax.convert_element_type(q, F32), final, picked)

                    picked = lax.fori_loop(0, visits, better, jnp.zeros((TILE, LANES), F32))
                    chosen[b, v, d, piece_rows, :] = picked.astype(BF16)

            each(visits, one_patch)
            each(visits, pick)

        for t in range(blocks):
            one_tile(t)

        for d in range(distinct):
            def templates(v):
                pl.when(below)(edge_copy(0, b, mine, v, d).start)
                pl.when(above)(edge_copy(1, b, mine, v, d).start)
                if b == last:
                    pl.when(me != v)(template_copy(b, mine, v, d).start)
                else:
                    template_copy(b, mine, v, d).start()

            each(visits, templates)
        if b == last:
            template_v[:, mine, pl.ds(TILE, rows), :] = chosen[b, me]

    @pl.when(owning)
    def _():
        for b in range(bands):
            reduce(b)

        def owners(v):
            for b in range(bands):
                if b == last:
                    pl.when(me != v)(owned_copy(b, mine, v).start)
                else:
                    owned_copy(b, mine, v).start()

        each(visits, owners)
        owned[mine] = patches[last, me]

    places = []
    for d in range(distinct):
        count = jnp.int32(0)
        found = [jnp.int32(0)] * cap
        for j in range(pieces):
            hit = seats[j] == slots[d]
            for k in range(cap):
                found[k] = found[k] + jnp.where(hit & (count == k), j, 0)
            count = count + jnp.where(hit, 1, 0)
        places += found
    order = jnp.zeros((1, LANES), jnp.int32)
    for k in range(pieces):
        order = order + jnp.where(iota((1, LANES), 1) == k, places[k], 0)
        for t in range(blocks):
            image_s[t, k] = image_v[places[k], pl.ds(t * TILE, TILE), :]
    order_out[...] = order
    for d in range(distinct):
        for t in range(blocks):
            lanes = pl.ds(t * cols, cols)
            for source, target in ((use, turned), (use_image, turned_image)):
                stack = [source[places[d * cap + k], :, lanes] for k in range(cap)]
                target[d, lanes, :] = jnp.transpose(jnp.concatenate(stack, axis=0))
    constants.wait()

    up_top = BASES // 2 * cols
    vertical = tables[pl.ds(up_top, 3 * rows), pl.ds(0, rows + 2 * TILE)]

    def across(c):
        return tables[pl.ds(c * cols, cols), pl.ds(0, cols)]

    wide_n = len(pairs) * TILE
    wide_b = BASES * TILE
    lines = small.shape[0]

    def kept(values):
        keep = (iota(values.shape, 0) & (TILE - 1)) == (iota(values.shape, 1) & (TILE - 1))
        return jnp.where(keep, values, 0.0)

    system = jnp.zeros((lines, LANES), F32)
    for d in range(distinct):
        for local in (False, True):
            for sides in range(3 if strips > 2 else 2):
                count = (halves - local) * rows + halves * sides * TILE

                @pl.when((owning == local) & (reach == sides + 1))
                def _():
                    if count:
                        wait_for(template_recv.at[d], count)

        template = jnp.concatenate([template_v[d, h] for h in range(halves)], axis=1)
        smooth = nn(vertical, template).astype(BF16)
        planes = [None] * BASES
        for c in range(3):
            taken = [a for a in range(BASES) if basis_cols[a] == c]
            product = nn(smooth[: len(taken) * rows], across(c)).astype(BF16)
            for a in taken:
                r = basis_rows[a]
                planes[a] = product[r * rows : (r + 1) * rows]
        for a in range(BASES):
            for t in range(blocks):
                basis[d, pl.ds(a * TILE, TILE), pl.ds(t * cols, cols)] = planes[a][
                    t * TILE : (t + 1) * TILE
                ]
        for n, (a, c) in enumerate(pairs):
            product = planes[a] * planes[c]
            for t in range(blocks):
                prods[pl.ds(n * TILE, TILE), pl.ds(t * cols, cols)] = product[
                    t * TILE : (t + 1) * TILE
                ]
        sums = jnp.concatenate([
            kept(nn(prods[...], turned[d])),
            kept(nn(basis[d], turned_image[d])),
            jnp.zeros((lines * TILE - wide_n - wide_b, cap * TILE), F32),
        ], axis=0)
        sums = jnp.sum(sums.reshape(lines, TILE, cap * TILE), axis=1)
        collect = jnp.right_shift(iota((cap * TILE, LANES), 0), 4) + d * cap
        collect = (collect == iota((cap * TILE, LANES), 1)).astype(F32).astype(BF16)
        gathered = nn(thirds(sums), collect)
        system = system + sum(gathered[k * lines : (k + 1) * lines] for k in range(3))
    small[...] = system
    exchanges = []
    for hop in range(1, strips):
        exchanges.append(pltpu.make_async_remote_copy(
            src_ref=small, dst_ref=small_in.at[hop - 1],
            send_sem=st_send, recv_sem=st_recv,
            device_id={"strip": lax.rem(strip + hop, strips)}, device_id_type=MESH,
        ))
    for copy in exchanges:
        copy.start()

    wide_c = 2 * wide_b
    column = iota((16, wide_c), 1)
    source = jnp.where(
        column < wide_b, jnp.right_shift(column, 4), jnp.right_shift(column - wide_b, 4) + 8
    )
    e3 = (source == iota((16, wide_c), 0)).astype(F32).astype(BF16)
    diagonal = iota((TILE, wide_c), 0) == (iota((TILE, wide_c), 1) & (TILE - 1))

    for local in (False, True):
        @pl.when(owning == local)
        def _():
            if halves - local:
                wait_for(owned_recv, (halves - local) * rows)
    for h in range(halves):
        coadd_out[:, pl.ds(h * LANES, LANES)] = owned[h]

    if exchanges:
        pltpu.make_async_copy(small_in, small_in, st_recv).wait()

    def line_of(n):
        value = small[pl.ds(n, 1), :]
        for hop in range(1, strips):
            value = value + small_in[hop - 1, pl.ds(n, 1), :]
        return value

    entry = {pairs[n]: line_of(n) + float(pairs[n][0] == pairs[n][1]) for n in range(len(pairs))}
    side = [line_of(len(pairs) + a) for a in range(BASES)]
    inverse = [None] * BASES
    for k in range(BASES):
        inverse[k] = 1.0 / entry[k, k]
        for i in range(k + 1, BASES):
            factor = entry[k, i] * inverse[k]
            for c in range(i, BASES):
                entry[i, c] = entry[i, c] - factor * entry[k, c]
            side[i] = side[i] - factor * side[k]
    for k in reversed(range(BASES)):
        for c in range(k + 1, BASES):
            side[k] = side[k] - entry[k, c] * side[c]
        side[k] = side[k] * inverse[k]
    found = jnp.zeros((8, LANES), F32)
    for a in range(BASES):
        found = found + jnp.where(iota((8, LANES), 0) == a, side[a], 0.0)
    high = found.astype(BF16).astype(F32)
    low = found - high
    both = jnp.concatenate([high, low], axis=0)[:, :pieces].astype(BF16)
    spread = tn(both, e3)
    for k in range(pieces):
        mixers[k // cap, pl.ds(k % cap * TILE, TILE), :] = jnp.where(
            diagonal, spread[k : k + 1], 0.0
        ).astype(BF16)

    for copy in exchanges:
        copy.wait_send()
    for local in (False, True):
        @pl.when(owning == local)
        def _():
            if halves - local:
                wait_for(sum_send, (halves - local) * parcel)
    for sides in range(3 if strips > 2 else 2):
        mains = (bands * visits - 1) * (distinct + 1) * rows
        edges = bands * visits * distinct * sides * TILE

        @pl.when(owning & (reach == sides + 1))
        def _():
            wait_for(template_send, mains + edges)


def finish(coadd_in, image_s, basis, mixers, order, coadd_out, diff_out, diff_v, places, out_sem):
    distinct = basis.shape[0]
    blocks, pieces, _, cols = image_s.shape
    cap = pieces // distinct
    bring = pltpu.make_async_copy(order, places, out_sem.at[1 + blocks])
    bring.start()
    stores = [pltpu.make_async_copy(coadd_in, coadd_out.at[0, 0], out_sem.at[0])]
    stores[0].start()
    bring.wait()
    for t in range(blocks):
        lanes = pl.ds(t * cols, cols)
        for d in range(distinct):
            planes = basis[d, :, lanes]
            fitted = nn(mixers[d], jnp.concatenate([planes, planes], axis=0))
            for k in range(cap):
                value = image_s[t, d * cap + k].astype(F32) - fitted[k * TILE : (k + 1) * TILE]
                diff_v[t, places[0, d * cap + k]] = value.astype(BF16)
        copy = pltpu.make_async_copy(
            diff_v.at[t], diff_out.at[0, :, pl.ds(t * TILE, TILE), :], out_sem.at[1 + t]
        )
        copy.start()
        stores.append(copy)
    for copy in stores:
        copy.wait()


def body(visits, strips, bands, images, mask_bits, visit_weight, intersection, patch_owner):
    _, pieces, rows, cols = images.shape
    blocks = rows // TILE
    halves = cols // LANES
    distinct = max(1, patch_owner.shape[0] // 2)
    cap = pieces // distinct
    taps = kernel_taps()
    width = -(-max(LANES, cols, rows + 2 * TILE) // LANES) * LANES
    tables = jnp.asarray(np.concatenate([
        np.pad(part, ((0, 0), (0, width - part.shape[1])))
        for part in (
            np.transpose(band_matrix(taps, cols, cols, HALF), (0, 2, 1)).reshape(3 * cols, cols),
            band_matrix(taps, rows, rows + 2 * TILE, HALF - TILE).reshape(3 * rows, -1),
        )
    ]), BF16)
    hbm = pl.BlockSpec(memory_space=pltpu.HBM)
    vmem = pl.BlockSpec(memory_space=pltpu.VMEM)
    dma = pltpu.SemaphoreType.DMA
    cross = intersection.reshape(1, pieces)
    others = max(1, strips - 1)
    parcel = distinct * 2 * rows + TILE
    lines = -(-(len(pairs) + BASES) // 8) * 8
    middle = pl.pallas_call(
        functools.partial(kernel, visits, strips, bands, distinct),
        out_shape=(
            jax.ShapeDtypeStruct((rows, cols), BF16),
            jax.ShapeDtypeStruct((blocks, pieces, TILE, cols), BF16),
            jax.ShapeDtypeStruct((distinct, BASES * TILE, blocks * cols), BF16),
            jax.ShapeDtypeStruct((distinct, cap * TILE, 2 * BASES * TILE), BF16),
            jax.ShapeDtypeStruct((1, LANES), jnp.int32),
        ),
        in_specs=[hbm, hbm, hbm, hbm, hbm, hbm],
        out_specs=(vmem, vmem, vmem, vmem, vmem),
        scratch_shapes=[
            pltpu.VMEM((pieces, rows, cols), jnp.int32),
            pltpu.VMEM((pieces, rows, cols), BF16),
            pltpu.VMEM(tables.shape, BF16),
            pltpu.VMEM((1, pieces), BF16),
            pltpu.SMEM((1, pieces), jnp.int32),
            pltpu.SMEM(patch_owner.shape, jnp.int32),
            pltpu.VMEM((pieces, TILE, blocks * cols), BF16),
            pltpu.VMEM((pieces, TILE, blocks * cols), BF16),
            pltpu.VMEM((distinct, blocks * cols, cap * TILE), BF16),
            pltpu.VMEM((distinct, blocks * cols, cap * TILE), BF16),
            pltpu.VMEM((halves, parcel, LANES), BF16),
            pltpu.VMEM((bands * visits * parcel, LANES), BF16),
            pltpu.VMEM((bands, visits, rows, LANES), BF16),
            pltpu.VMEM((bands, visits, distinct, rows, LANES), BF16),
            pltpu.VMEM((distinct, halves, rows + 2 * TILE, LANES), BF16),
            pltpu.VMEM((halves, rows, LANES), BF16),
            pltpu.VMEM((len(pairs) * TILE, blocks * cols), BF16),
            pltpu.VMEM((lines, LANES), F32),
            pltpu.VMEM((others, lines, LANES), F32),
            dma((3,)),
            dma((2, 2)),
            dma,
            dma,
            dma((bands,)),
            dma,
            dma((distinct,)),
            dma,
            dma,
            dma,
        ],
        compiler_params=pltpu.CompilerParams(
            collective_id=0, has_side_effects=True, vmem_limit_bytes=40_000_000
        ),
        name="coadd_solve",
    )(*(
        pltpu.with_memory_space_constraint(part, pltpu.HBM)
        for part in (images, mask_bits, visit_weight, cross, patch_owner, tables)
    ))
    return pl.pallas_call(
        finish,
        out_shape=(
            jax.ShapeDtypeStruct((1, 1, rows, cols), BF16),
            jax.ShapeDtypeStruct(images.shape, BF16),
        ),
        in_specs=[vmem, vmem, vmem, vmem, vmem],
        out_specs=(hbm, hbm),
        scratch_shapes=[
            pltpu.VMEM((blocks, pieces, TILE, cols), BF16),
            pltpu.SMEM((1, LANES), jnp.int32),
            dma((2 + blocks,)),
        ],
        compiler_params=pltpu.CompilerParams(vmem_limit_bytes=40 * 1024 * 1024),
        name="difference",
    )(*middle)


def solution(mesh):
    in_specs = (
        P("band", ("groups", "visit"), "strip", None),
        P("band", ("groups", "visit"), "strip", None),
        P("band", ("groups", "visit")),
        P(("groups", "visit"), None),
        P("groups"),
    )
    out_specs = (
        P("band", ("groups", "visit"), "strip", None),
        P("band", ("groups", "visit"), "strip", None),
    )
    step = functools.partial(
        body, mesh.shape["visit"], mesh.shape["strip"], mesh.shape["band"]
    )
    return jax.shard_map(step, mesh=mesh, in_specs=in_specs, out_specs=out_specs, check_vma=False)
```

time: 23.2 us -> 20.2 us (0.87)
  Pallas kernels: 21.7 us -> 19.4 us
  local copies, waits for them, and re-layouts: 0.66 us -> 0 us
    pallas_call x1, Pallas kernels: 20.5 us -> 17.9 us  [body(): pl.pallas_call(functools.partial(kernel, visits, strips, bands, distinct)...]
    unnamed x6 -> x0, local copies, waits for them, and re-layouts: 0.66 us -> none
    pallas_call x1, Pallas kernels: 1.18 us -> 1.57 us  [body(): pl.pallas_call(finish, out_shape=(jax.ShapeDtypeStruct((1, 1, rows, cols)...]
where the time goes in v2:
time: 20.2 us; the launch traced here: 20.1 us
  Pallas kernels  19.4 us (96%)
  between operations  0.64 us (3%)
    pallas_call x1, Pallas kernels, body(): pl.pallas_call(functools.partial(kernel, visits, strips, bands, distinct)...  17.9 us
    pallas_call x1, Pallas kernels, body(): pl.pallas_call(finish, out_shape=(jax.ShapeDtypeStruct((1, 1, rows, cols)...  1.57 us

profile of v2, /device:TPU:0, one launch (start us, length us, event | category | flops | bytes accessed | tf_op | source)
XLA Modules:
  0.0 20.1 jit_solution(16970637757475365900)
XLA Ops:
  0.6 17.9 %coadd_solve.1 = (bf16[64,256]{1,0:T(8,128)(2,1)S(1)}, bf16[4,16,16,256]{3,2,1,0:T(8,128)(2,1)S(1)}, bf16[2,96,1024]{2,1,0:T(8,128)(2,1)S(1)}, bf16[2,128,192]{2,1,0:T(8,128)(2,1)S(1)}, s32[1,128]{1,0:T(1,128)S(1)}) custom-call(bf16[1,16,64,256]{3,2,1,0:T(8,128)(2,1)} %images.1, s32[1,16,64,256]{3,2,1,0:T(8,128)} %masks.1, bf16[1,16]{1,0:T(2,128)(2,1)} %weight_in.1, ...), custom_call_target="tpu_custom_call" | custom-call | tf_op jit(solution)/shard_map/coadd_solve/pallas_call | solution.py:590
  18.5 1.6 %difference.1 = (bf16[1,1,64,256]{3,2,1,0:T(8,128)(2,1)}, bf16[1,16,64,256]{3,2,1,0:T(8,128)(2,1)}) custom-call(bf16[64,256]{1,0:T(8,128)(2,1)S(1)} %get-tuple-element.7.coadd_in, bf16[4,16,16,256]{3,2,1,0:T(8,128)(2,1)S(1)} %get-tuple-element.8.image_s, bf16[2,96,1024]{2,1,0:T(8,128)(2,1)S(1)} %get-tuple-element.9.basis, ...), custom_call_target="tpu_custom_call" | custom-call | tf_op jit(solution)/shard_map/difference/pallas_call | solution.py:640

commit v3 on v2

--- a/solution.py
+++ b/solution.py
@@ -77,19 +77,20 @@
     images, masks, weight_in, cross_in, owner_in, table_in,
     coadd_out, image_s, basis, mixers, order_out,
     mask_v, image_v, tables, weight, cross, owner, use, use_image, turned, turned_image, send, recv,
-    patches, chosen, template_v, owned, prods, small, small_in,
+    patches, chosen, template_v, owned, prods, small, small_in, lined,
     first_sem, in_sem, const_sem, sum_send, sum_recv, template_send, template_recv, owned_recv,
     st_send, st_recv,
 ):
     pieces, rows, cols = images.shape[1:]
     blocks = rows // TILE
-    chunk = rows // in_sem.shape[1]
+    chunks = in_sem.shape[1]
+    chunk = rows // chunks
     span = pieces * TILE
     cap = pieces // distinct
     halves = cols // LANES
     lead = (visits - halves) // 2
     last = bands - 1
-    sheet = distinct * 2 * rows
+    sheet = distinct * 2 * chunk
     parcel = sheet + TILE
     me = lax.axis_index("visit")
     strip = lax.axis_index("strip")
@@ -109,6 +110,16 @@
     for copy in firsts:
         copy.start()
 
+    loads = []
+    for k in range(chunks):
+        part = pl.ds(k * chunk, chunk)
+        loads.append((
+            pltpu.make_async_copy(masks.at[0, :, part, :], mask_v.at[:, part, :], in_sem.at[0, k]),
+            pltpu.make_async_copy(images.at[0, :, part, :], image_v.at[:, part, :], in_sem.at[1, k]),
+        ))
+        for copy in loads[k]:
+            copy.start()
+
     barrier = pltpu.get_barrier_semaphore()
 
     def greet(v, hop, b):
@@ -161,15 +172,6 @@
         for hop in range(1, strips):
             greet(me, hop, band)
 
-    loads = []
-    for k in range(rows // chunk):
-        part = pl.ds(k * chunk, chunk)
-        loads.append((
-            pltpu.make_async_copy(masks.at[0, :, part, :], mask_v.at[:, part, :], in_sem.at[0, k]),
-            pltpu.make_async_copy(images.at[0, :, part, :], image_v.at[:, part, :], in_sem.at[1, k]),
-        ))
-        for copy in loads[k]:
-            copy.start()
     constants = pltpu.make_async_copy(table_in, tables, const_sem)
     constants.start()
 
@@ -204,42 +206,29 @@
     for d in range(distinct):
         names = names + jnp.where(iota((TILE, LANES), 0) == d, slots[d], 0)
     for h in range(halves):
-        send[h, pl.ds(sheet, TILE), :] = names.astype(F32).astype(BF16)
-
-    for t in range(blocks):
-        if t * TILE % chunk == 0:
-            for copy in loads[t * TILE // chunk]:
-                copy.wait()
-        piece_rows = pl.ds(t * TILE, TILE)
-        lanes = pl.ds(t * cols, cols)
-        usable = ((mask_v[:, piece_rows, :].reshape(span, cols) & 3) != 3).astype(F32).astype(BF16)
-        masked = usable * image_v[:, piece_rows, :].reshape(span, cols)
-        use[:, :, lanes] = usable.reshape(pieces, TILE, cols)
-        use_image[:, :, lanes] = masked.reshape(pieces, TILE, cols)
-        for part, value in enumerate((masked, usable)):
-            total = nn(adder, value).astype(BF16)
-            for d in range(distinct):
-                for h in range(halves):
-                    send[h, pl.ds((d * 2 + part) * rows + t * TILE, TILE), :] = total[
-                        d * TILE : (d + 1) * TILE, h * LANES : (h + 1) * LANES
-                    ]
-
-    def parcel_at(b, v):
-        return pl.multiple_of((b * visits + v) * parcel, TILE)
+        send[h, 0, pl.ds(sheet, TILE), :] = names.astype(F32).astype(BF16)
+
+    def parcel_at(b, c, v):
+        return pl.multiple_of(((b * chunks + c) * visits + v) * parcel, TILE)
+
+    def size(c):
+        return parcel if c == 0 else sheet
 
     def some(count):
         return recv.at[pl.ds(0, count), :]
 
-    def sum_copy(h, b):
+    def sum_copy(h, b, c):
         return pltpu.make_async_remote_copy(
-            src_ref=send.at[h], dst_ref=recv.at[pl.ds(parcel_at(b, me), parcel), :],
-            send_sem=sum_send, recv_sem=sum_recv.at[b],
+            src_ref=send.at[h, c, pl.ds(0, size(c)), :],
+            dst_ref=recv.at[pl.ds(parcel_at(b, c, me), size(c)), :],
+            send_sem=sum_send, recv_sem=sum_recv.at[b, c],
             device_id={"visit": lead + h, "band": last}, device_id_type=MESH,
         )
 
-    def template_copy(b, h, v, d):
+    def template_copy(b, h, v, d, c):
         return pltpu.make_async_remote_copy(
-            src_ref=chosen.at[b, v, d], dst_ref=template_v.at[d, h, pl.ds(TILE, rows), :],
+            src_ref=chosen.at[b, v, d, pl.ds(c * chunk, chunk), :],
+            dst_ref=template_v.at[d, h, pl.ds(TILE + c * chunk, chunk), :],
             send_sem=template_send, recv_sem=template_recv.at[d],
             device_id={"visit": v, "band": b}, device_id_type=MESH,
         )
@@ -264,15 +253,38 @@
     def wait_for(sem, count):
         pltpu.make_async_copy(some(count), some(count), sem).wait()
 
+    def partial(c):
+        for copy in loads[c]:
+            copy.wait()
+        for t in range(c * chunk // TILE, (c + 1) * chunk // TILE):
+            piece_rows = pl.ds(t * TILE, TILE)
+            lanes = pl.ds(t * cols, cols)
+            usable = (mask_v[:, piece_rows, :].reshape(span, cols) & 3) != 3
+            usable = usable.astype(F32).astype(BF16)
+            masked = usable * image_v[:, piece_rows, :].reshape(span, cols)
+            use[:, :, lanes] = usable.reshape(pieces, TILE, cols)
+            use_image[:, :, lanes] = masked.reshape(pieces, TILE, cols)
+            for part, value in enumerate((masked, usable)):
+                total = nn(adder, value).astype(BF16)
+                for d in range(distinct):
+                    for h in range(halves):
+                        at = (d * 2 + part) * chunk + t * TILE - c * chunk
+                        send[h, c, pl.ds(at, TILE), :] = total[
+                            d * TILE : (d + 1) * TILE, h * LANES : (h + 1) * LANES
+                        ]
+
     met = jnp.where(
         owning, visits * bands * reach - 1 + strips - reach, halves * reach + strips - 1
     )
-    pl.semaphore_wait(barrier, met)
-    for b in range(bands):
-        for h in range(halves):
-            @pl.when((band == b) & jnp.logical_not(owning & (mine == h)))
-            def _():
-                sum_copy(h, b).start()
+    for c in range(chunks):
+        partial(c)
+        if c == 0:
+            pl.semaphore_wait(barrier, met)
+        for b in range(bands):
+            for h in range(halves):
+                @pl.when((band == b) & jnp.logical_not(owning & (mine == h)))
+                def _():
+                    sum_copy(h, b, c).start()
 
     @pl.when(jnp.logical_not(above))
     def _():
@@ -284,17 +296,18 @@
             (distinct, halves, TILE, LANES), BF16
         )
 
-    def reduce(b):
+    def reduce(b, c):
         if b == last:
-            recv[pl.ds(parcel_at(b, me), parcel), :] = send[mine]
-        wait_for(sum_recv.at[b], (visits if b != last else visits - 1) * parcel)
+            recv[pl.ds(parcel_at(b, c, me), parcel), :] = send[mine, c]
+        wait_for(sum_recv.at[b, c], (visits if b != last else visits - 1) * size(c))
 
         def id_tile(v, d):
-            names = recv[pl.ds(parcel_at(b, v) + sheet, TILE), :].astype(F32)
+            names = recv[pl.ds(parcel_at(b, 0, v) + sheet, TILE), :].astype(F32)
             return jnp.broadcast_to(names[d : d + 1], (TILE, LANES))
 
         def value(v, d, part, t):
-            start = pl.multiple_of(parcel_at(b, v) + (d * 2 + part) * rows + t * TILE, TILE)
+            at = (d * 2 + part) * chunk + t * TILE - c * chunk
+            start = pl.multiple_of(parcel_at(b, c, v) + at, TILE)
             return recv[pl.ds(start, TILE), :].astype(F32)
 
         def one_tile(t):
@@ -351,26 +364,28 @@
             each(visits, one_patch)
             each(visits, pick)
 
-        for t in range(blocks):
+        for t in range(c * chunk // TILE, (c + 1) * chunk // TILE):
             one_tile(t)
 
         for d in range(distinct):
             def templates(v):
-                pl.when(below)(edge_copy(0, b, mine, v, d).start)
-                pl.when(above)(edge_copy(1, b, mine, v, d).start)
+                if c == chunks - 1:
+                    pl.when(below)(edge_copy(0, b, mine, v, d).start)
+                if c == 0:
+                    pl.when(above)(edge_copy(1, b, mine, v, d).start)
                 if b == last:
-                    pl.when(me != v)(template_copy(b, mine, v, d).start)
+                    pl.when(me != v)(template_copy(b, mine, v, d, c).start)
                 else:
-                    template_copy(b, mine, v, d).start()
+                    template_copy(b, mine, v, d, c).start()
 
             each(visits, templates)
-        if b == last:
-            template_v[:, mine, pl.ds(TILE, rows), :] = chosen[b, me]
 
     @pl.when(owning)
     def _():
-        for b in range(bands):
-            reduce(b)
+        for c in range(chunks):
+            for b in range(bands):
+                reduce(b, c)
+        template_v[:, mine, pl.ds(TILE, rows), :] = chosen[last, me]
 
         def owners(v):
             for b in range(bands):
@@ -414,7 +429,7 @@
 
     wide_n = len(pairs) * TILE
     wide_b = BASES * TILE
-    lines = small.shape[0]
+    lines = lined.shape[0]
 
     def kept(values):
         keep = (iota(values.shape, 0) & (TILE - 1)) == (iota(values.shape, 1) & (TILE - 1))
@@ -461,7 +476,11 @@
         collect = (collect == iota((cap * TILE, LANES), 1)).astype(F32).astype(BF16)
         gathered = nn(thirds(sums), collect)
         system = system + sum(gathered[k * lines : (k + 1) * lines] for k in range(3))
-    small[...] = system
+    groups = lines // 8
+    small[...] = sum(
+        pltpu.roll(system[g * 8 : (g + 1) * 8], g * pieces, 1) if g else system[:8]
+        for g in range(groups)
+    )
     exchanges = []
     for hop in range(1, strips):
         exchanges.append(pltpu.make_async_remote_copy(
@@ -491,11 +510,14 @@
     if exchanges:
         pltpu.make_async_copy(small_in, small_in, st_recv).wait()
 
+    full = small[...]
+    for hop in range(1, strips):
+        full = full + small_in[hop - 1]
+    for g in range(groups):
+        lined[pl.ds(g * 8, 8), :] = pltpu.roll(full, LANES - g * pieces, 1) if g else full
+
     def line_of(n):
-        value = small[pl.ds(n, 1), :]
-        for hop in range(1, strips):
-            value = value + small_in[hop - 1, pl.ds(n, 1), :]
-        return value
+        return lined[pl.ds(n, 1), :]
 
     entry = {pairs[n]: line_of(n) + float(pairs[n][0] == pairs[n][1]) for n in range(len(pairs))}
     side = [line_of(len(pairs) + a) for a in range(BASES)]
@@ -529,7 +551,7 @@
         @pl.when(owning == local)
         def _():
             if halves - local:
-                wait_for(sum_send, (halves - local) * parcel)
+                wait_for(sum_send, (halves - local) * sum(size(c) for c in range(chunks)))
     for sides in range(3 if strips > 2 else 2):
         mains = (bands * visits - 1) * (distinct + 1) * rows
         edges = bands * visits * distinct * sides * TILE
@@ -539,15 +561,13 @@
             wait_for(template_send, mains + edges)
 
 
-def finish(coadd_in, image_s, basis, mixers, order, coadd_out, diff_out, diff_v, places, out_sem):
+def finish(coadd_in, image_s, basis, mixers, order, coadd_out, diff_out, diff_v, out_sem):
     distinct = basis.shape[0]
     blocks, pieces, _, cols = image_s.shape
     cap = pieces // distinct
-    bring = pltpu.make_async_copy(order, places, out_sem.at[1 + blocks])
-    bring.start()
     stores = [pltpu.make_async_copy(coadd_in, coadd_out.at[0, 0], out_sem.at[0])]
     stores[0].start()
-    bring.wait()
+    places = [order[0, k] for k in range(pieces)]
     for t in range(blocks):
         lanes = pl.ds(t * cols, cols)
         for d in range(distinct):
@@ -555,7 +575,7 @@
             fitted = nn(mixers[d], jnp.concatenate([planes, planes], axis=0))
             for k in range(cap):
                 value = image_s[t, d * cap + k].astype(F32) - fitted[k * TILE : (k + 1) * TILE]
-                diff_v[t, places[0, d * cap + k]] = value.astype(BF16)
+                diff_v[t, places[d * cap + k]] = value.astype(BF16)
         copy = pltpu.make_async_copy(
             diff_v.at[t], diff_out.at[0, :, pl.ds(t * TILE, TILE), :], out_sem.at[1 + t]
         )
@@ -585,7 +605,8 @@
     dma = pltpu.SemaphoreType.DMA
     cross = intersection.reshape(1, pieces)
     others = max(1, strips - 1)
-    parcel = distinct * 2 * rows + TILE
+    chunks = 2
+    parcel = distinct * 2 * rows // chunks + TILE
     lines = -(-(len(pairs) + BASES) // 8) * 8
     middle = pl.pallas_call(
         functools.partial(kernel, visits, strips, bands, distinct),
@@ -609,20 +630,21 @@
             pltpu.VMEM((pieces, TILE, blocks * cols), BF16),
             pltpu.VMEM((distinct, blocks * cols, cap * TILE), BF16),
             pltpu.VMEM((distinct, blocks * cols, cap * TILE), BF16),
-            pltpu.VMEM((halves, parcel, LANES), BF16),
-            pltpu.VMEM((bands * visits * parcel, LANES), BF16),
+            pltpu.VMEM((halves, chunks, parcel, LANES), BF16),
+            pltpu.VMEM((bands * chunks * visits * parcel, LANES), BF16),
             pltpu.VMEM((bands, visits, rows, LANES), BF16),
             pltpu.VMEM((bands, visits, distinct, rows, LANES), BF16),
             pltpu.VMEM((distinct, halves, rows + 2 * TILE, LANES), BF16),
             pltpu.VMEM((halves, rows, LANES), BF16),
             pltpu.VMEM((len(pairs) * TILE, blocks * cols), BF16),
+            pltpu.VMEM((8, LANES), F32),
+            pltpu.VMEM((others, 8, LANES), F32),
             pltpu.VMEM((lines, LANES), F32),
-            pltpu.VMEM((others, lines, LANES), F32),
             dma((3,)),
-            dma((2, 2)),
+            dma((2, chunks)),
             dma,
             dma,
-            dma((bands,)),
+            dma((bands, chunks)),
             dma,
             dma((distinct,)),
             dma,
@@ -647,8 +669,7 @@
         out_specs=(hbm, hbm),
         scratch_shapes=[
             pltpu.VMEM((blocks, pieces, TILE, cols), BF16),
-            pltpu.SMEM((1, LANES), jnp.int32),
-            dma((2 + blocks,)),
+            dma((1 + blocks,)),
         ],
         compiler_params=pltpu.CompilerParams(vmem_limit_bytes=40 * 1024 * 1024),
         name="difference",

time: 20.2 us -> 19.5 us (0.965)
  Pallas kernels: 19.4 us -> 18.7 us
    pallas_call x1, Pallas kernels: 1.57 us -> 1.05 us  [body(): pl.pallas_call(finish, out_shape=(jax.ShapeDtypeStruct((1, 1, rows, cols)...]
    pallas_call x1, Pallas kernels: 17.9 us -> 17.6 us  [body(): pl.pallas_call(functools.partial(kernel, visits, strips, bands, distinct)...]
where the time goes in v3:
time: 19.5 us; the launch traced here: 19.3 us
  Pallas kernels  18.7 us (96%)
  between operations  0.64 us (3%)
    pallas_call x1, Pallas kernels, body(): pl.pallas_call(functools.partial(kernel, visits, strips, bands, distinct)...  17.6 us
    pallas_call x1, Pallas kernels, body(): pl.pallas_call(finish, out_shape=(jax.ShapeDtypeStruct((1, 1, rows, cols)...  1.05 us

profile of v3, /device:TPU:0, one launch (start us, length us, event | category | flops | bytes accessed | tf_op | source)
XLA Modules:
  0.0 19.3 jit_solution(6536923146859348379)
XLA Ops:
  0.6 17.6 %coadd_solve.1 = (bf16[64,256]{1,0:T(8,128)(2,1)S(1)}, bf16[4,16,16,256]{3,2,1,0:T(8,128)(2,1)S(1)}, bf16[2,96,1024]{2,1,0:T(8,128)(2,1)S(1)}, bf16[2,128,192]{2,1,0:T(8,128)(2,1)S(1)}, s32[1,128]{1,0:T(1,128)S(1)}) custom-call(bf16[1,16,64,256]{3,2,1,0:T(8,128)(2,1)} %images.1, s32[1,16,64,256]{3,2,1,0:T(8,128)} %masks.1, bf16[1,16]{1,0:T(2,128)(2,1)} %weight_in.1, ...), custom_call_target="tpu_custom_call" | custom-call | tf_op jit(solution)/shard_map/coadd_solve/pallas_call | solution.py:611
  18.3 1.0 %difference.1 = (bf16[1,1,64,256]{3,2,1,0:T(8,128)(2,1)}, bf16[1,16,64,256]{3,2,1,0:T(8,128)(2,1)}) custom-call(bf16[64,256]{1,0:T(8,128)(2,1)S(1)} %get-tuple-element.7.coadd_in, bf16[4,16,16,256]{3,2,1,0:T(8,128)(2,1)S(1)} %get-tuple-element.8.image_s, bf16[2,96,1024]{2,1,0:T(8,128)(2,1)S(1)} %get-tuple-element.9.basis, ...), custom_call_target="tpu_custom_call" | custom-call | tf_op jit(solution)/shard_map/difference/pallas_call | solution.py:662

commit v4 on v3

--- a/solution.py
+++ b/solution.py
@@ -83,7 +83,8 @@
 ):
     pieces, rows, cols = images.shape[1:]
     blocks = rows // TILE
-    chunks = in_sem.shape[1]
+    chunks = sum_recv.shape[1]
+    parts = in_sem.shape[1]
     chunk = rows // chunks
     span = pieces * TILE
     cap = pieces // distinct
@@ -98,6 +99,7 @@
     above = strip > 0
     below = strip < strips - 1
     mine = me - lead
+    late = me * 2 >= visits
     central = (me >= lead) & (me < lead + halves)
     owning = central & (band == last)
     reach = 1 + above.astype(jnp.int32) + below.astype(jnp.int32)
@@ -111,8 +113,8 @@
         copy.start()
 
     loads = []
-    for k in range(chunks):
-        part = pl.ds(k * chunk, chunk)
+    for k in range(parts):
+        part = pl.ds(k * rows // parts, rows // parts)
         loads.append((
             pltpu.make_async_copy(masks.at[0, :, part, :], mask_v.at[:, part, :], in_sem.at[0, k]),
             pltpu.make_async_copy(images.at[0, :, part, :], image_v.at[:, part, :], in_sem.at[1, k]),
@@ -217,28 +219,28 @@
     def some(count):
         return recv.at[pl.ds(0, count), :]
 
-    def sum_copy(h, b, c):
+    def sum_copy(h, c):
         return pltpu.make_async_remote_copy(
             src_ref=send.at[h, c, pl.ds(0, size(c)), :],
-            dst_ref=recv.at[pl.ds(parcel_at(b, c, me), size(c)), :],
-            send_sem=sum_send, recv_sem=sum_recv.at[b, c],
+            dst_ref=recv.at[pl.ds(parcel_at(band, c, me), size(c)), :],
+            send_sem=sum_send, recv_sem=sum_recv.at[band, c],
             device_id={"visit": lead + h, "band": last}, device_id_type=MESH,
         )
 
-    def template_copy(b, h, v, d, c):
+    def template_copy(b, h, v, c):
         return pltpu.make_async_remote_copy(
-            src_ref=chosen.at[b, v, d, pl.ds(c * chunk, chunk), :],
-            dst_ref=template_v.at[d, h, pl.ds(TILE + c * chunk, chunk), :],
-            send_sem=template_send, recv_sem=template_recv.at[d],
+            src_ref=chosen.at[b, v, :, pl.ds(c * chunk, chunk), :],
+            dst_ref=template_v.at[h, :, pl.ds(TILE + c * chunk, chunk), :],
+            send_sem=template_send, recv_sem=template_recv,
             device_id={"visit": v, "band": b}, device_id_type=MESH,
         )
 
-    def edge_copy(way, b, h, v, d):
+    def edge_copy(way, b, h, v):
         step, source, target = ((1, rows - TILE, 0), (strips - 1, 0, rows + TILE))[way]
         return pltpu.make_async_remote_copy(
-            src_ref=chosen.at[b, v, d, pl.ds(source, TILE), :],
-            dst_ref=template_v.at[d, h, pl.ds(target, TILE), :],
-            send_sem=template_send, recv_sem=template_recv.at[d],
+            src_ref=chosen.at[b, v, :, pl.ds(source, TILE), :],
+            dst_ref=template_v.at[h, :, pl.ds(target, TILE), :],
+            send_sem=template_send, recv_sem=template_recv,
             device_id={"visit": v, "strip": lax.rem(strip + step, strips), "band": b},
             device_id_type=MESH,
         )
@@ -254,8 +256,9 @@
         pltpu.make_async_copy(some(count), some(count), sem).wait()
 
     def partial(c):
-        for copy in loads[c]:
-            copy.wait()
+        if c * parts % chunks == 0:
+            for copy in loads[c * parts // chunks]:
+                copy.wait()
         for t in range(c * chunk // TILE, (c + 1) * chunk // TILE):
             piece_rows = pl.ds(t * TILE, TILE)
             lanes = pl.ds(t * cols, cols)
@@ -280,21 +283,28 @@
         partial(c)
         if c == 0:
             pl.semaphore_wait(barrier, met)
-        for b in range(bands):
-            for h in range(halves):
-                @pl.when((band == b) & jnp.logical_not(owning & (mine == h)))
-                def _():
-                    sum_copy(h, b, c).start()
+        for k in range(halves):
+            h = jnp.where(late, k, halves - 1 - k)
+            pl.when(jnp.logical_not(owning & (mine == h)))(sum_copy(h, c).start)
 
     @pl.when(jnp.logical_not(above))
     def _():
-        template_v[:, :, pl.ds(0, TILE), :] = jnp.zeros((distinct, halves, TILE, LANES), BF16)
+        template_v[:, :, pl.ds(0, TILE), :] = jnp.zeros((halves, distinct, TILE, LANES), BF16)
 
     @pl.when(jnp.logical_not(below))
     def _():
         template_v[:, :, pl.ds(rows + TILE, TILE), :] = jnp.zeros(
-            (distinct, halves, TILE, LANES), BF16
+            (halves, distinct, TILE, LANES), BF16
         )
+
+    def visit_all(act, others_only=False):
+        if visits > 4:
+            each(visits - others_only, lambda k: act(lax.rem(me + others_only + k, visits)))
+            return
+        hops = sorted(range(visits), key=lambda k: (abs(k - visits // 2), -k))
+        for k in hops:
+            if k or not others_only:
+                act(lax.rem(me + jnp.where(late, visits - k, k), visits))
 
     def reduce(b, c):
         if b == last:
@@ -367,34 +377,26 @@
         for t in range(c * chunk // TILE, (c + 1) * chunk // TILE):
             one_tile(t)
 
-        for d in range(distinct):
-            def templates(v):
-                if c == chunks - 1:
-                    pl.when(below)(edge_copy(0, b, mine, v, d).start)
-                if c == 0:
-                    pl.when(above)(edge_copy(1, b, mine, v, d).start)
-                if b == last:
-                    pl.when(me != v)(template_copy(b, mine, v, d, c).start)
-                else:
-                    template_copy(b, mine, v, d, c).start()
-
-            each(visits, templates)
+        if c == chunks - 1:
+            @pl.when(below)
+            def _():
+                visit_all(lambda v: edge_copy(0, b, mine, v).start())
+
+        if c == 0:
+            @pl.when(above)
+            def _():
+                visit_all(lambda v: edge_copy(1, b, mine, v).start())
+
+        visit_all(lambda v: template_copy(b, mine, v, c).start(), b == last)
 
     @pl.when(owning)
     def _():
         for c in range(chunks):
             for b in range(bands):
                 reduce(b, c)
-        template_v[:, mine, pl.ds(TILE, rows), :] = chosen[last, me]
-
-        def owners(v):
-            for b in range(bands):
-                if b == last:
-                    pl.when(me != v)(owned_copy(b, mine, v).start)
-                else:
-                    owned_copy(b, mine, v).start()
-
-        each(visits, owners)
+        template_v[mine, :, pl.ds(TILE, rows), :] = chosen[last, me]
+        for b in range(bands):
+            visit_all(lambda v: owned_copy(b, mine, v).start(), b == last)
         owned[mine] = patches[last, me]
 
     places = []
@@ -431,52 +433,58 @@
     wide_b = BASES * TILE
     lines = lined.shape[0]
 
-    def kept(values):
-        keep = (iota(values.shape, 0) & (TILE - 1)) == (iota(values.shape, 1) & (TILE - 1))
-        return jnp.where(keep, values, 0.0)
-
-    system = jnp.zeros((lines, LANES), F32)
+    for local in (False, True):
+        for sides in range(3 if strips > 2 else 2):
+            count = distinct * ((halves - local) * rows + halves * sides * TILE)
+
+            @pl.when((owning == local) & (reach == sides + 1))
+            def _():
+                if count:
+                    wait_for(template_recv, count)
+
+    corner = iota((1, TILE, cap * TILE), 1) == (iota((1, TILE, cap * TILE), 2) & (TILE - 1))
+    smooth = nn(vertical, jnp.concatenate(
+        [template_v[h, d] for d in range(distinct) for h in range(halves)], axis=1
+    )).astype(BF16)
+    planes = [[None] * BASES for _ in range(distinct)]
+    for c in range(3):
+        taken = [a for a in range(BASES) if basis_cols[a] == c]
+        height = len(taken) * rows
+        product = nn(jnp.concatenate(
+            [smooth[:height, d * cols : (d + 1) * cols] for d in range(distinct)], axis=0
+        ), across(c)).astype(BF16)
+        for d in range(distinct):
+            for a in taken:
+                top = d * height + basis_rows[a] * rows
+                planes[d][a] = product[top : top + rows]
     for d in range(distinct):
-        for local in (False, True):
-            for sides in range(3 if strips > 2 else 2):
-                count = (halves - local) * rows + halves * sides * TILE
-
-                @pl.when((owning == local) & (reach == sides + 1))
-                def _():
-                    if count:
-                        wait_for(template_recv.at[d], count)
-
-        template = jnp.concatenate([template_v[d, h] for h in range(halves)], axis=1)
-        smooth = nn(vertical, template).astype(BF16)
-        planes = [None] * BASES
-        for c in range(3):
-            taken = [a for a in range(BASES) if basis_cols[a] == c]
-            product = nn(smooth[: len(taken) * rows], across(c)).astype(BF16)
-            for a in taken:
-                r = basis_rows[a]
-                planes[a] = product[r * rows : (r + 1) * rows]
         for a in range(BASES):
             for t in range(blocks):
-                basis[d, pl.ds(a * TILE, TILE), pl.ds(t * cols, cols)] = planes[a][
+                basis[d, pl.ds(a * TILE, TILE), pl.ds(t * cols, cols)] = planes[d][a][
                     t * TILE : (t + 1) * TILE
                 ]
         for n, (a, c) in enumerate(pairs):
-            product = planes[a] * planes[c]
+            product = planes[d][a] * planes[d][c]
             for t in range(blocks):
-                prods[pl.ds(n * TILE, TILE), pl.ds(t * cols, cols)] = product[
+                prods[d, pl.ds(n * TILE, TILE), pl.ds(t * cols, cols)] = product[
                     t * TILE : (t + 1) * TILE
                 ]
+
+    groups = lines // 8
+    folded = []
+    for d in range(distinct):
         sums = jnp.concatenate([
-            kept(nn(prods[...], turned[d])),
-            kept(nn(basis[d], turned_image[d])),
+            nn(prods[d], turned[d]),
+            nn(basis[d], turned_image[d]),
             jnp.zeros((lines * TILE - wide_n - wide_b, cap * TILE), F32),
-        ], axis=0)
-        sums = jnp.sum(sums.reshape(lines, TILE, cap * TILE), axis=1)
-        collect = jnp.right_shift(iota((cap * TILE, LANES), 0), 4) + d * cap
-        collect = (collect == iota((cap * TILE, LANES), 1)).astype(F32).astype(BF16)
-        gathered = nn(thirds(sums), collect)
-        system = system + sum(gathered[k * lines : (k + 1) * lines] for k in range(3))
-    groups = lines // 8
+        ], axis=0).reshape(lines, TILE, cap * TILE)
+        folded.append(jnp.sum(jnp.where(corner, sums, 0.0), axis=1))
+    collect = jnp.concatenate([
+        jnp.right_shift(iota((cap * TILE, LANES), 0), 4) + d * cap for d in range(distinct)
+    ], axis=0)
+    collect = (collect == iota(collect.shape, 1)).astype(F32).astype(BF16)
+    gathered = nn(thirds(jnp.concatenate(folded, axis=1)), collect)
+    system = sum(gathered[k * lines : (k + 1) * lines] for k in range(3))
     small[...] = sum(
         pltpu.roll(system[g * 8 : (g + 1) * 8], g * pieces, 1) if g else system[:8]
         for g in range(groups)
@@ -634,19 +642,19 @@
             pltpu.VMEM((bands * chunks * visits * parcel, LANES), BF16),
             pltpu.VMEM((bands, visits, rows, LANES), BF16),
             pltpu.VMEM((bands, visits, distinct, rows, LANES), BF16),
-            pltpu.VMEM((distinct, halves, rows + 2 * TILE, LANES), BF16),
+            pltpu.VMEM((halves, distinct, rows + 2 * TILE, LANES), BF16),
             pltpu.VMEM((halves, rows, LANES), BF16),
-            pltpu.VMEM((len(pairs) * TILE, blocks * cols), BF16),
+            pltpu.VMEM((distinct, len(pairs) * TILE, blocks * cols), BF16),
             pltpu.VMEM((8, LANES), F32),
             pltpu.VMEM((others, 8, LANES), F32),
             pltpu.VMEM((lines, LANES), F32),
             dma((3,)),
-            dma((2, chunks)),
+            dma((2, 2)),
             dma,
             dma,
             dma((bands, chunks)),
             dma,
-            dma((distinct,)),
+            dma,
             dma,
             dma,
             dma,

time: 19.5 us -> 18.6 us (0.954)
  Pallas kernels: 18.7 us -> 17.8 us
    pallas_call x1, Pallas kernels: 17.6 us -> 16.8 us  [body(): pl.pallas_call(functools.partial(kernel, visits, strips, bands, distinct)...]
where the time goes in v4:
time: 18.6 us; the launch traced here: 18.5 us
  Pallas kernels  17.8 us (96%)
  between operations  0.64 us (3%)
    pallas_call x1, Pallas kernels, body(): pl.pallas_call(functools.partial(kernel, visits, strips, bands, distinct)...  16.8 us
    pallas_call x1, Pallas kernels, body(): pl.pallas_call(finish, out_shape=(jax.ShapeDtypeStruct((1, 1, rows, cols)...  1.05 us

profile of v4, /device:TPU:0, one launch (start us, length us, event | category | flops | bytes accessed | tf_op | source)
XLA Modules:
  0.0 18.5 jit_solution(7137987767391701327)
XLA Ops:
  0.6 16.8 %coadd_solve.1 = (bf16[64,256]{1,0:T(8,128)(2,1)S(1)}, bf16[4,16,16,256]{3,2,1,0:T(8,128)(2,1)S(1)}, bf16[2,96,1024]{2,1,0:T(8,128)(2,1)S(1)}, bf16[2,128,192]{2,1,0:T(8,128)(2,1)S(1)}, s32[1,128]{1,0:T(1,128)S(1)}) custom-call(bf16[1,16,64,256]{3,2,1,0:T(8,128)(2,1)} %images.1, s32[1,16,64,256]{3,2,1,0:T(8,128)} %masks.1, bf16[1,16]{1,0:T(2,128)(2,1)} %weight_in.1, ...), custom_call_target="tpu_custom_call" | custom-call | tf_op jit(solution)/shard_map/coadd_solve/pallas_call | solution.py:619
  17.4 1.0 %difference.1 = (bf16[1,1,64,256]{3,2,1,0:T(8,128)(2,1)}, bf16[1,16,64,256]{3,2,1,0:T(8,128)(2,1)}) custom-call(bf16[64,256]{1,0:T(8,128)(2,1)S(1)} %get-tuple-element.7.coadd_in, bf16[4,16,16,256]{3,2,1,0:T(8,128)(2,1)S(1)} %get-tuple-element.8.image_s, bf16[2,96,1024]{2,1,0:T(8,128)(2,1)S(1)} %get-tuple-element.9.basis, ...), custom_call_target="tpu_custom_call" | custom-call | tf_op jit(solution)/shard_map/difference/pallas_call | solution.py:670

commit v5 on v4

--- a/solution.py
+++ b/solution.py
@@ -104,6 +104,51 @@
     owning = central & (band == last)
     reach = 1 + above.astype(jnp.int32) + below.astype(jnp.int32)
 
+    def visit_all(act, others_only=False):
+        if visits > 4:
+            each(visits - others_only, lambda k: act(lax.rem(me + others_only + k, visits)))
+            return
+        hops = sorted(range(visits), key=lambda k: (abs(k - visits // 2), -k))
+        for k in hops:
+            if k or not others_only:
+                act(lax.rem(me + jnp.where(late, visits - k, k), visits))
+
+    barrier = pltpu.get_barrier_semaphore()
+
+    def greet(v, hop, b):
+        target = {"visit": v, "strip": lax.rem(strip + hop, strips), "band": b}
+        pl.semaphore_signal(barrier, inc=1, device_id=target, device_id_type=MESH)
+
+    def near(hop, step):
+        if hop == 0:
+            step()
+        elif hop == 1 and strips == 2:
+            step()
+        elif hop == 1:
+            pl.when(below)(step)
+        elif hop == strips - 1:
+            pl.when(above)(step)
+
+    def adjoining(hop):
+        if hop in (0, 1) and strips == 2:
+            return jnp.bool_(True)
+        return below if hop == 1 else (above if hop == strips - 1 else jnp.bool_(False))
+
+    @pl.when(owning)
+    def _():
+        for b in range(bands):
+            visit_all(lambda v: greet(v, 0, b), b == last)
+        for hop in sorted({1 % strips, strips - 1} - {0}):
+            def greet_owners():
+                for h in range(halves):
+                    greet(lead + h, hop, last)
+
+            near(hop, greet_owners)
+            if strips > 2:
+                pl.when(jnp.logical_not(adjoining(hop)))(functools.partial(greet, me, hop, band))
+        for hop in range(2, strips - 1):
+            greet(me, hop, band)
+
     firsts = [
         pltpu.make_async_copy(cross_in, cross, first_sem.at[0]),
         pltpu.make_async_copy(owner_in, owner, first_sem.at[1]),
@@ -121,47 +166,6 @@
         ))
         for copy in loads[k]:
             copy.start()
-
-    barrier = pltpu.get_barrier_semaphore()
-
-    def greet(v, hop, b):
-        target = {"visit": v, "strip": lax.rem(strip + hop, strips), "band": b}
-        pl.semaphore_signal(barrier, inc=1, device_id=target, device_id_type=MESH)
-
-    def near(hop, step):
-        if hop == 0:
-            step()
-        elif hop == 1 and strips == 2:
-            step()
-        elif hop == 1:
-            pl.when(below)(step)
-        elif hop == strips - 1:
-            pl.when(above)(step)
-
-    def adjoining(hop):
-        if hop in (0, 1) and strips == 2:
-            return jnp.bool_(True)
-        return below if hop == 1 else (above if hop == strips - 1 else jnp.bool_(False))
-
-    @pl.when(owning)
-    def _():
-        for hop in sorted({0, 1 % strips, strips - 1}):
-            def greet_strip():
-                def greet_visit(v):
-                    for b in range(bands):
-                        if hop == 0 and b == last:
-                            pl.when(me != v)(functools.partial(greet, v, hop, b))
-                        else:
-                            greet(v, hop, b)
-
-                each(visits, greet_visit)
-
-            near(hop, greet_strip)
-        for hop in range(2, strips - 1):
-            greet(me, hop, band)
-        for hop in sorted({1 % strips, strips - 1} - {0}):
-            if strips > 2:
-                pl.when(jnp.logical_not(adjoining(hop)))(functools.partial(greet, me, hop, band))
 
     @pl.when(jnp.logical_not(owning))
     def _():
@@ -277,7 +281,7 @@
                         ]
 
     met = jnp.where(
-        owning, visits * bands * reach - 1 + strips - reach, halves * reach + strips - 1
+        owning, visits * bands * reach - 1 + strips - reach, halves + strips - 1
     )
     for c in range(chunks):
         partial(c)
@@ -296,15 +300,6 @@
         template_v[:, :, pl.ds(rows + TILE, TILE), :] = jnp.zeros(
             (halves, distinct, TILE, LANES), BF16
         )
-
-    def visit_all(act, others_only=False):
-        if visits > 4:
-            each(visits - others_only, lambda k: act(lax.rem(me + others_only + k, visits)))
-            return
-        hops = sorted(range(visits), key=lambda k: (abs(k - visits // 2), -k))
-        for k in hops:
-            if k or not others_only:
-                act(lax.rem(me + jnp.where(late, visits - k, k), visits))
 
     def reduce(b, c):
         if b == last:
@@ -391,8 +386,8 @@
 
     @pl.when(owning)
     def _():
-        for c in range(chunks):
-            for b in range(bands):
+        for b in range(bands):
+            for c in range(chunks):
                 reduce(b, c)
         template_v[mine, :, pl.ds(TILE, rows), :] = chosen[last, me]
         for b in range(bands):
@@ -585,12 +580,11 @@
                 value = image_s[t, d * cap + k].astype(F32) - fitted[k * TILE : (k + 1) * TILE]
                 diff_v[t, places[d * cap + k]] = value.astype(BF16)
         copy = pltpu.make_async_copy(
-            diff_v.at[t], diff_out.at[0, :, pl.ds(t * TILE, TILE), :], out_sem.at[1 + t]
+            diff_v.at[t], diff_out.at[0, :, pl.ds(t * TILE, TILE), :], out_sem.at[1]
         )
         copy.start()
-        stores.append(copy)
-    for copy in stores:
-        copy.wait()
+    stores[0].wait()
+    pltpu.make_async_copy(diff_v, diff_v, out_sem.at[1]).wait()
 
 
 def body(visits, strips, bands, images, mask_bits, visit_weight, intersection, patch_owner):
@@ -613,7 +607,7 @@
     dma = pltpu.SemaphoreType.DMA
     cross = intersection.reshape(1, pieces)
     others = max(1, strips - 1)
-    chunks = 2
+    chunks = 4
     parcel = distinct * 2 * rows // chunks + TILE
     lines = -(-(len(pairs) + BASES) // 8) * 8
     middle = pl.pallas_call(
@@ -677,7 +671,7 @@
         out_specs=(hbm, hbm),
         scratch_shapes=[
             pltpu.VMEM((blocks, pieces, TILE, cols), BF16),
-            dma((1 + blocks,)),
+            dma((2,)),
         ],
         compiler_params=pltpu.CompilerParams(vmem_limit_bytes=40 * 1024 * 1024),
         name="difference",

time: 18.6 us -> 18.2 us (0.978)
  Pallas kernels: 17.8 us -> 17.5 us
    pallas_call x1, Pallas kernels: 16.8 us -> 16.4 us  [body(): pl.pallas_call(functools.partial(kernel, visits, strips, bands, distinct)...]
where the time goes in v5:
time: 18.2 us; the launch traced here: 18.1 us
  Pallas kernels  17.5 us (96%)
  between operations  0.64 us (4%)
    pallas_call x1, Pallas kernels, body(): pl.pallas_call(functools.partial(kernel, visits, strips, bands, distinct)...  16.4 us
    pallas_call x1, Pallas kernels, body(): pl.pallas_call(finish, out_shape=(jax.ShapeDtypeStruct((1, 1, rows, cols)...  1.02 us

profile of v5, /device:TPU:0, one launch (start us, length us, event | category | flops | bytes accessed | tf_op | source)
XLA Modules:
  0.0 18.1 jit_solution(11903565658522002998)
XLA Ops:
  0.6 16.4 %coadd_solve.1 = (bf16[64,256]{1,0:T(8,128)(2,1)S(1)}, bf16[4,16,16,256]{3,2,1,0:T(8,128)(2,1)S(1)}, bf16[2,96,1024]{2,1,0:T(8,128)(2,1)S(1)}, bf16[2,128,192]{2,1,0:T(8,128)(2,1)S(1)}, s32[1,128]{1,0:T(1,128)S(1)}) custom-call(bf16[1,16,64,256]{3,2,1,0:T(8,128)(2,1)} %images.1, s32[1,16,64,256]{3,2,1,0:T(8,128)} %masks.1, bf16[1,16]{1,0:T(2,128)(2,1)} %weight_in.1, ...), custom_call_target="tpu_custom_call" | custom-call | tf_op jit(solution)/shard_map/coadd_solve/pallas_call | solution.py:613
  17.1 1.0 %difference.1 = (bf16[1,1,64,256]{3,2,1,0:T(8,128)(2,1)}, bf16[1,16,64,256]{3,2,1,0:T(8,128)(2,1)}) custom-call(bf16[64,256]{1,0:T(8,128)(2,1)S(1)} %get-tuple-element.7.coadd_in, bf16[4,16,16,256]{3,2,1,0:T(8,128)(2,1)S(1)} %get-tuple-element.8.image_s, bf16[2,96,1024]{2,1,0:T(8,128)(2,1)S(1)} %get-tuple-element.9.basis, ...), custom_call_target="tpu_custom_call" | custom-call | tf_op jit(solution)/shard_map/difference/pallas_call | solution.py:664
